TPU v7x, 32 devices: a whole 2x2x4 slice. The times are simulated.
32 devices in a mesh: dp: 8 (over z, y), tensor: 4 (over x, core).
Axes of the slice: x: 2, y: 2, z: 4, core: 2. Of those that a mesh axis runs over, the one named last changes fastest.
Arguments:
- frames_in: bfloat16 [12000, 1536], P(('dp', 'tensor')), may hold values from -6 to 6
- text_states: bfloat16 [512, 1536], P('dp'), may hold values from -6 to 6
- adapter_pick: int32 [8], P('dp'), may hold values from 0 to 7
- out_grad: bfloat16 [12000, 1536], P('dp'), may hold values from -6 to 6
- norm_gain: float32 [3, 1536], replicated, may hold values from 0.1 to 1.9
- norm_bias: float32 [3, 1536], replicated, may hold values from -3 to 3
- col_w: bfloat16 [6, 1536, 1536], P(None, None, 'tensor'), may hold values from -0.15625 to 0.15625
- col_a: bfloat16 [6, 8, 1536, 16], replicated, may hold values from -0.15625 to 0.15625
- col_b: bfloat16 [6, 8, 16, 1536], P(None, None, None, 'tensor'), may hold values from -1.5 to 1.5
- row_w: bfloat16 [2, 1536, 1536], P(None, 'tensor'), may hold values from -0.625 to 0.625
- row_a: bfloat16 [2, 8, 1536, 16], P(None, None, 'tensor'), may hold values from -0.625 to 0.625
- row_b: bfloat16 [2, 8, 16, 1536], replicated, may hold values from -1.5 to 1.5
- mlp_in: bfloat16 [1536, 6144], P(None, 'tensor'), may hold values from -0.15625 to 0.15625
- mlp_in_a: bfloat16 [8, 1536, 16], replicated, may hold values from -0.15625 to 0.15625
- mlp_in_b: bfloat16 [8, 16, 6144], P(None, None, 'tensor'), may hold values from -1.5 to 1.5
- mlp_out: bfloat16 [6144, 1536], P('tensor'), may hold values from -0.078125 to 0.078125
- mlp_out_a: bfloat16 [8, 6144, 16], P(None, 'tensor'), may hold values from -0.078125 to 0.078125
- mlp_out_b: bfloat16 [8, 16, 1536], replicated, may hold values from -1.5 to 1.5
Outputs:
- block_out: bfloat16 [12000, 1536], P(('dp', 'tensor'))
- frames_grad: float32 [12000, 1536], P(('dp', 'tensor'))
- text_grad: float32 [512, 1536], P(('dp', 'tensor'))
- col_a_grad: float32 [6, 8, 1536, 16], replicated
- col_b_grad: float32 [6, 8, 16, 1536], P(None, None, None, 'tensor')
- row_a_grad: float32 [2, 8, 1536, 16], P(None, None, 'tensor')
- row_b_grad: float32 [2, 8, 16, 1536], replicated
- mlp_in_a_grad: float32 [8, 1536, 16], replicated
- mlp_in_b_grad: float32 [8, 16, 6144], P(None, None, 'tensor')
- mlp_out_a_grad: float32 [8, 6144, 16], P(None, 'tensor')
- mlp_out_b_grad: float32 [8, 16, 1536], replicated
All inputs are finite; a program needn't handle non-finite values.
Results may differ from a plain program's by a relative error of at most 0.034.
Values may be sent and summed in bfloat16 or wider, within the bound.
A program may use at most 256 MiB of HBM per device.

v0:
```python
from functools import partial

import jax
import jax.numpy as jnp
from jax import lax
from jax.sharding import PartitionSpec as P

HEAD = 64


HIGHEST_PRECISION = lax.Precision.HIGHEST
EPSILON = 1e-05


def dot_low(former, latter):
    return jnp.dot(former, latter, preferred_element_type=jnp.float32)


def dot_high(former, latter):
    return jnp.dot(former, latter, precision=HIGHEST_PRECISION, preferred_element_type=jnp.float32)


def times_trans(former, latter):
    return lax.dot_general(
        former, latter, (((1,), (1,)), ((), ())), preferred_element_type=jnp.float32
    )


def normed(values_in, scale_vec, shift_vec):
    row_mean = jnp.mean(values_in, axis=-1, keepdims=True)
    centred = values_in - row_mean
    variance = jnp.mean(centred * centred, axis=-1, keepdims=True)
    return centred * lax.rsqrt(variance + EPSILON) * scale_vec + shift_vec


def causal_scores(queries, all_keys, first_row):
    scores = (
        jnp.einsum("qhe,khe->hqk", queries, all_keys, preferred_element_type=jnp.float32) * 0.125
    )
    query_pos = first_row + lax.iota(jnp.int32, queries.shape[0])
    key_pos = lax.iota(jnp.int32, all_keys.shape[0])
    return jnp.where(key_pos[None, None, :] <= query_pos[None, :, None], scores, -1e30)


def softmax_back(attn_probs, grad_probs):
    weighted = jnp.sum(attn_probs * grad_probs, axis=-1, keepdims=True)
    return (attn_probs * (grad_probs - weighted)).astype(jnp.bfloat16)


def self_forward(queries, all_keys, all_values, first_row):
    scores = causal_scores(queries, all_keys, first_row)
    row_max = jnp.max(scores, axis=-1, keepdims=True)
    log_total = row_max + jnp.log(jnp.sum(jnp.exp(scores - row_max), axis=-1, keepdims=True))
    probs_full = jnp.exp(scores - log_total)
    attn_mixed = jnp.einsum(
        "hqk,khe->qhe",
        probs_full.astype(jnp.bfloat16),
        all_values,
        preferred_element_type=jnp.float32,
    )
    return (attn_mixed, log_total, probs_full)


def self_backward(queries, all_keys, all_values, grad_mixed, attn_probs):
    grad_probs = jnp.einsum(
        "qhe,khe->hqk", grad_mixed, all_values, preferred_element_type=jnp.float32
    )
    grad_values = jnp.einsum(
        "hqk,qhe->khe",
        attn_probs.astype(jnp.bfloat16),
        grad_mixed,
        preferred_element_type=jnp.float32,
    )
    grad_scores = softmax_back(attn_probs, grad_probs)
    grad_queries = (
        jnp.einsum("hqk,khe->qhe", grad_scores, all_keys, preferred_element_type=jnp.float32)
        * 0.125
    )
    grad_keys = (
        jnp.einsum("hqk,qhe->khe", grad_scores, queries, preferred_element_type=jnp.float32) * 0.125
    )
    return (grad_queries, grad_keys, grad_values)


def into_slots(gradient, slot_mask, slot_axis):
    new_shape = [1] * (gradient.ndim + 1)
    new_shape[slot_axis] = slot_mask.shape[0]
    return jnp.expand_dims(gradient, slot_axis) * slot_mask.reshape(new_shape)


def flatten_all(pieces):
    return jnp.concatenate([piece.reshape(-1) for piece in pieces])


def unflatten_all(vector, pieces):
    results = []
    offset = 0
    for piece in pieces:
        results.append(vector[offset : offset + piece.size].reshape(piece.shape))
        offset = offset + piece.size
    return results


def local(
    frames_in,
    text_states,
    adapter_pick,
    out_grad,
    norm_gain,
    norm_bias,
    col_w,
    col_a,
    col_b,
    row_w,
    row_a,
    row_b,
    mlp_in,
    mlp_in_a,
    mlp_in_b,
    mlp_out,
    mlp_out_a,
    mlp_out_b,
):
    adapter_index = adapter_pick[0]

    def chosen(stacked, slot_axis):
        return lax.dynamic_index_in_dim(stacked, adapter_index, slot_axis, keepdims=False)

    col_down = chosen(col_a, 1)
    col_up = chosen(col_b, 1)
    row_down = chosen(row_a, 1)
    row_up = chosen(row_b, 1)
    in_down = chosen(mlp_in_a, 0)
    in_up = chosen(mlp_in_b, 0)
    out_down = chosen(mlp_out_a, 0)
    out_up = chosen(mlp_out_b, 0)
    row_share = frames_in.astype(jnp.float32)
    share_rows = row_share.shape[0]
    tensor_rank = lax.axis_index("tensor")
    local_width = col_w.shape[2]
    heads_local = local_width // HEAD

    def project(source, proj_slot):
        low_rank = dot_low(source, col_down[proj_slot])
        projected = dot_low(source, col_w[proj_slot]) + dot_high(
            low_rank, col_up[proj_slot].astype(jnp.float32)
        )
        return (
            projected.astype(jnp.bfloat16).reshape(source.shape[0], heads_local, HEAD),
            low_rank,
        )

    def row_term(source, proj_slot):
        low_rank = dot_low(source, row_down[proj_slot])
        return dot_low(source, row_w[proj_slot]) + dot_high(
            low_rank, row_up[proj_slot].astype(jnp.float32)
        )

    def row_back(source, grad_full, proj_slot):
        back_rank = times_trans(grad_full, row_up[proj_slot])
        grad_source = times_trans(grad_full, row_w[proj_slot]) + dot_high(
            back_rank, row_down[proj_slot].T
        )
        grad_down = dot_high(source.T, back_rank)
        grad_up = dot_high(dot_low(source, row_down[proj_slot]).T, grad_full)
        return (grad_source.astype(jnp.bfloat16), grad_down, grad_up)

    def adapter_grads(source, grad_out, proj_slot, low_rank):
        back_rank = times_trans(grad_out, col_up[proj_slot])
        return (back_rank, dot_high(source.T, back_rank), dot_high(low_rank.T, grad_out))

    def source_grad(grad_out, back_rank, proj_slot):
        return times_trans(grad_out, col_w[proj_slot]) + dot_high(back_rank, col_down[proj_slot].T)

    norm_one = lax.all_gather(
        normed(row_share, norm_gain[0], norm_bias[0]).astype(jnp.bfloat16),
        "tensor",
        axis=0,
        tiled=True,
    )
    length = norm_one.shape[0]
    queries, query_rank = project(norm_one, 0)
    all_keys, key_rank = project(norm_one, 1)
    all_values, value_rank = project(norm_one, 2)
    block_count = max(1, length // 512)
    block_rows = length // block_count
    starts = jnp.arange(block_count, dtype=jnp.int32) * block_rows
    query_blocks = queries.reshape(block_count, block_rows, heads_local, HEAD)

    def forward_again(pieces):
        return self_forward(pieces[0], all_keys, all_values, pieces[1])[:2]

    attn_mixed, saved_blocks = lax.map(forward_again, (query_blocks, starts))
    attended = attn_mixed.reshape(length, local_width).astype(jnp.bfloat16)
    first = row_share + lax.psum_scatter(
        row_term(attended, 0), "tensor", scatter_dimension=0, tiled=True
    )
    norm_two = lax.all_gather(
        normed(first, norm_gain[1], norm_bias[1]).astype(jnp.bfloat16), "tensor", axis=0, tiled=True
    )
    cross_queries, cross_query_rank = project(norm_two, 3)
    cross_keys, cross_key_rank = project(text_states, 4)
    cross_values, cross_value_rank = project(text_states, 5)
    cross_scores = (
        jnp.einsum("qhe,khe->hqk", cross_queries, cross_keys, preferred_element_type=jnp.float32)
        * 0.125
    )
    cross_probs = jax.nn.softmax(cross_scores, axis=-1)
    cross_low = cross_probs.astype(jnp.bfloat16)
    cross_mixed = jnp.einsum(
        "hqk,khe->qhe", cross_low, cross_values, preferred_element_type=jnp.float32
    )
    cross_mixed = cross_mixed.reshape(length, local_width).astype(jnp.bfloat16)
    second = first + lax.psum_scatter(
        row_term(cross_mixed, 1), "tensor", scatter_dimension=0, tiled=True
    )
    norm_three = lax.all_gather(
        normed(second, norm_gain[2], norm_bias[2]).astype(jnp.bfloat16),
        "tensor",
        axis=0,
        tiled=True,
    )
    up_rank = dot_low(norm_three, in_down)
    pre = dot_low(norm_three, mlp_in) + dot_high(up_rank, in_up.astype(jnp.float32))
    hidden = jax.nn.gelu(pre, approximate=False).astype(jnp.bfloat16)
    row_part = hidden
    low_rank = dot_low(row_part, out_down)
    third = second + lax.psum_scatter(
        (dot_low(row_part, mlp_out) + dot_high(low_rank, out_up.astype(jnp.float32))).astype(
            jnp.bfloat16
        ),
        "tensor",
        scatter_dimension=0,
        tiled=True,
    ).astype(jnp.float32)
    block_out = third.astype(jnp.bfloat16)
    grad_res = lax.dynamic_slice_in_dim(out_grad, tensor_rank * share_rows, share_rows, 0).astype(
        jnp.float32
    )
    down_back = times_trans(out_grad, out_up)
    grad_hidden = times_trans(out_grad, mlp_out) + dot_high(down_back, out_down.T)
    grad_out_down = dot_high(hidden.T, down_back)
    grad_out_up = dot_high(dot_low(hidden, out_down).T, out_grad)
    gelu_back = jax.vjp(partial(jax.nn.gelu, approximate=False), pre)[1]
    grad_pre = gelu_back(grad_hidden)[0].astype(jnp.bfloat16)
    up_back = times_trans(grad_pre, in_up)
    grad_in_down = dot_high(norm_three.T, up_back)
    grad_in_up = dot_high(up_rank.T, grad_pre)
    row_part = grad_pre
    back_part = up_back
    grad_norm_three = lax.psum_scatter(
        times_trans(row_part, mlp_in) + dot_high(back_part, in_down.T),
        "tensor",
        scatter_dimension=0,
        tiled=True,
    )
    norm_back_three = jax.vjp(
        lambda values_in: normed(values_in, norm_gain[2], norm_bias[2]), second
    )[1]
    grad_res = grad_res + norm_back_three(grad_norm_three)[0]
    grad_cross_full = lax.all_gather(grad_res.astype(jnp.bfloat16), "tensor", axis=0, tiled=True)
    grad_cross_mixed, grad_cross_down, grad_cross_up = row_back(cross_mixed, grad_cross_full, 1)
    grad_cross_mixed = grad_cross_mixed.reshape(length, heads_local, HEAD)
    grad_cross_probs = jnp.einsum(
        "qhe,khe->hqk", grad_cross_mixed, cross_values, preferred_element_type=jnp.float32
    )
    grad_cross_values = jnp.einsum(
        "hqk,qhe->khe", cross_low, grad_cross_mixed, preferred_element_type=jnp.float32
    )
    grad_cross_scores = softmax_back(cross_probs, grad_cross_probs)
    grad_cross_queries = (
        jnp.einsum(
            "hqk,khe->qhe", grad_cross_scores, cross_keys, preferred_element_type=jnp.float32
        )
        * 0.125
    )
    grad_cross_keys = (
        jnp.einsum(
            "hqk,qhe->khe", grad_cross_scores, cross_queries, preferred_element_type=jnp.float32
        )
        * 0.125
    )
    text_rows = text_states.shape[0]
    grad_cq = grad_cross_queries.reshape(length, local_width).astype(jnp.bfloat16)
    grad_ck = grad_cross_keys.reshape(text_rows, local_width).astype(jnp.bfloat16)
    grad_cv = grad_cross_values.reshape(text_rows, local_width).astype(jnp.bfloat16)
    back_three, down_three, up_three = adapter_grads(norm_two, grad_cq, 3, cross_query_rank)
    back_four, down_four, up_four = adapter_grads(text_states, grad_ck, 4, cross_key_rank)
    back_five, down_five, up_five = adapter_grads(text_states, grad_cv, 5, cross_value_rank)
    grad_norm_part = source_grad(grad_cq, back_three, 3)
    grad_text_part = source_grad(grad_ck, back_four, 4) + source_grad(grad_cv, back_five, 5)
    grad_norm_two, text_grad = (
        lax.psum_scatter(
            grad_norm_part.astype(jnp.bfloat16), "tensor", scatter_dimension=0, tiled=True
        ).astype(jnp.float32),
        lax.psum_scatter(
            grad_text_part.astype(jnp.bfloat16), "tensor", scatter_dimension=0, tiled=True
        ).astype(jnp.float32),
    )
    norm_back_two = jax.vjp(lambda values_in: normed(values_in, norm_gain[1], norm_bias[1]), first)[
        1
    ]
    grad_res = grad_res + norm_back_two(grad_norm_two)[0]
    grad_self_full = lax.all_gather(grad_res.astype(jnp.bfloat16), "tensor", axis=0, tiled=True)
    grad_attended, grad_self_down, grad_self_up = row_back(attended, grad_self_full, 0)
    grad_blocks = grad_attended.reshape(block_count, block_rows, heads_local, HEAD)

    def back_step(carried, pieces):
        attn_probs = jnp.exp(causal_scores(pieces[0], all_keys, pieces[3]) - pieces[2])
        grad_queries, grad_keys, grad_values = self_backward(
            pieces[0], all_keys, all_values, pieces[1], attn_probs
        )
        return ((carried[0] + grad_keys, carried[1] + grad_values), grad_queries)

    empty_grad = jnp.zeros((length, heads_local, HEAD), jnp.float32)
    (key_grads, value_grads), query_grads = lax.scan(
        back_step, (empty_grad, empty_grad), (query_blocks, grad_blocks, saved_blocks, starts)
    )
    grad_q = query_grads.reshape(length, local_width).astype(jnp.bfloat16)
    grad_k = key_grads.reshape(length, local_width).astype(jnp.bfloat16)
    grad_v = value_grads.reshape(length, local_width).astype(jnp.bfloat16)
    back_zero, down_zero, up_zero = adapter_grads(norm_one, grad_q, 0, query_rank)
    back_one, down_one, up_one = adapter_grads(norm_one, grad_k, 1, key_rank)
    back_two, down_two, up_two = adapter_grads(norm_one, grad_v, 2, value_rank)
    summed = jnp.zeros((share_rows * lax.axis_size("tensor"), norm_one.shape[1]), jnp.float32)
    for grad_out, back_rank, proj_slot in (
        (grad_q, back_zero, 0),
        (grad_k, back_one, 1),
        (grad_v, back_two, 2),
    ):
        back_part = back_rank
        summed = summed + source_grad(grad_out, back_part, proj_slot)
    grad_norm_one = lax.psum_scatter(
        summed.astype(jnp.bfloat16), "tensor", scatter_dimension=0, tiled=True
    ).astype(jnp.float32)
    norm_back_one = jax.vjp(
        lambda values_in: normed(values_in, norm_gain[0], norm_bias[0]), row_share
    )[1]
    frames_grad = grad_res + norm_back_one(grad_norm_one)[0]
    slot_mask = (lax.iota(jnp.int32, col_a.shape[1]) == adapter_index).astype(jnp.float32)
    col_up_local = jnp.stack([up_zero, up_one, up_two, up_three, up_four, up_five])
    row_down_local = jnp.stack([grad_self_down, grad_cross_down])
    col_down_part = jnp.stack([down_zero, down_one, down_two, down_three, down_four, down_five])
    row_up_part = jnp.stack([grad_self_up, grad_cross_up])
    own_parts = [
        into_slots(col_up_local, slot_mask, 1),
        into_slots(row_down_local, slot_mask, 1),
        into_slots(grad_in_up, slot_mask, 0),
        into_slots(grad_out_down, slot_mask, 0),
    ]
    common_parts = [
        into_slots(col_down_part, slot_mask, 1),
        into_slots(row_up_part, slot_mask, 1),
        into_slots(grad_in_down, slot_mask, 0),
        into_slots(grad_out_up, slot_mask, 0),
    ]
    own_share, common_share = (
        lax.psum_scatter(flatten_all(own_parts), "dp", scatter_dimension=0, tiled=True),
        lax.psum_scatter(flatten_all(common_parts), "dp", scatter_dimension=0, tiled=True),
    )
    common_share = lax.psum(common_share.astype(jnp.bfloat16), "tensor").astype(jnp.float32)
    own_whole, common_whole = (
        lax.all_gather(own_share.astype(jnp.bfloat16), "dp", axis=0, tiled=True).astype(
            own_share.dtype
        ),
        lax.all_gather(common_share.astype(jnp.bfloat16), "dp", axis=0, tiled=True).astype(
            common_share.dtype
        ),
    )
    col_b_grad, row_a_grad, mlp_in_b_grad, mlp_out_a_grad = unflatten_all(own_whole, own_parts)
    col_a_grad, row_b_grad, mlp_in_a_grad, mlp_out_b_grad = unflatten_all(
        common_whole, common_parts
    )
    return (
        block_out,
        frames_grad,
        text_grad,
        col_a_grad,
        col_b_grad,
        row_a_grad,
        row_b_grad,
        mlp_in_a_grad,
        mlp_in_b_grad,
        mlp_out_a_grad,
        mlp_out_b_grad,
    )


def solution(mesh):
    return jax.shard_map(
        local,
        mesh=mesh,
        in_specs=(
            P(("dp", "tensor"), None),
            P("dp", None),
            P("dp"),
            P("dp", None),
            P(),
            P(),
            P(None, None, "tensor"),
            P(),
            P(None, None, None, "tensor"),
            P(None, "tensor", None),
            P(None, None, "tensor", None),
            P(),
            P(None, "tensor"),
            P(),
            P(None, None, "tensor"),
            P("tensor", None),
            P(None, "tensor", None),
            P(),
        ),
        out_specs=(
            P(("dp", "tensor"), None),
            P(("dp", "tensor"), None),
            P(("dp", "tensor"), None),
            P(),
            P(None, None, None, "tensor"),
            P(None, None, "tensor", None),
            P(),
            P(),
            P(None, None, "tensor"),
            P(None, "tensor", None),
            P(),
        ),
        check_vma=False,
    )
```

profile of v0, /device:TPU:13, one launch (start us, length us, event | category | flops | bytes accessed | tf_op | source)
XLA Modules:
  0.0 1958.5 jit_solution(2530468602131154666)
XLA Ops:
  15.7 37.9 %all-gather.17.cloned.1.call-done = bf16[4,375,1536]{2,1,0:T(8,128)(2,1)} async-done(((bf16[1,375,1536]{2,1,0:T(8,128)(2,1)}), bf16[4,375,1536]{2,1,0:T(8,128)(2,1)}) %all-gather.17.cloned.1.call-update) | async-done | bytes 4608016 | tf_op jit(solution)/shard_map/all_gather | solution.py:175
  104.3 82.0 %while.27 = (s32[]{:T(128)}, bf16[2,750,6,64]{1,3,2,0:T(8,128)(2,1)}, f32[2,6,750,1]{2,1,3,0:T(8,128)}, s32[2]{0:T(128)S(1)}, bf16[2,750,6,64]{1,3,2,0:T(8,128)(...) while((s32[]{:T(128)}, bf16[2,750,6,64]{1,3,2,0:T(8,128)(2,1)}, ...), condition=%wide.region_5.6_spmd, body=%wide.region_2.5_spmd.sunk | while | flops 1803371264 | bytes 95340064 | solution.py:193
  106.2 13.1 fusion.396
  119.4 12.6 exponential_reduce_fusion.2
  132.0 13.3 fusion.397
  147.2 13.1 fusion.396
  160.3 12.6 exponential_reduce_fusion.2
  173.0 13.3 fusion.397
  207.2 81.8 %fusion = f32[376,1536]{1,0:T(8,128)} fusion(f32[1500,1536]{1,0:T(8,128)} %convolution_add_fusion.9), kind=kCustom, calls=%all-reduce-scatter | all-reduce-scatter fusion | flops 2310145 | bytes 11526656
  318.5 30.5 %all-gather.19.cloned.1.call-done = bf16[4,375,1536]{2,1,0:T(8,128)(2,1)} async-done(((bf16[1,375,1536]{2,1,0:T(8,128)(2,1)}), bf16[4,375,1536]{2,1,0:T(8,128)(2,1)}) %all-gather.19.cloned.1.call-update) | async-done | bytes 4608016 | tf_op jit(solution)/shard_map/all_gather | solution.py:198
  383.7 81.7 %fusion.1 = f32[376,1536]{1,0:T(8,128)} fusion(f32[1500,1536]{1,0:T(8,128)} %convolution_add_fusion.8), kind=kCustom, calls=%all-reduce-scatter.1 | all-reduce-scatter fusion | flops 2310145 | bytes 11526656
  489.4 13.2 fusion.252
  502.6 22.1 %all-gather.21.cloned.1.call-done = bf16[4,375,1536]{2,1,0:T(8,128)(2,1)} async-done(((bf16[1,375,1536]{2,1,0:T(8,128)(2,1)}), bf16[4,375,1536]{2,1,0:T(8,128)(2,1)}) %all-gather.21.cloned.1.call-update) | async-done | bytes 4608016 | tf_op jit(solution)/shard_map/all_gather | solution.py:217
  543.7 28.4 %multiply_convert_fusion.1 = (bf16[1500,1536]{1,0:T(8,128)(2,1)}, f32[1500,1536]{1,0:T(8,128)}, f32[1500,1536]{1,0:T(8,128)}) fusion(f32[1500,1536]{1,0:T(8,128)S(1)} %fusion.250, f32[1500,16]{0,1:T(8,128)S(1)} %fusion.166, bf16[8,16,1536]{2,1,0:T(8,128)(2,1)} %param.36, s32[]{:T(128)S(6)} %select_n.26), kind=kOutput, calls=%fused_computation.64 | convolution fusion | flops 594432000 | bytes 32401156 | tf_op jit(solution)/shard_map/dot_general | solution.py:20
  603.3 81.7 %fusion.3 = f32[376,1536]{1,0:T(8,128)} fusion(f32[1500,1536]{1,0:T(8,128)} %convolution_add_fusion.4), kind=kCustom, calls=%all-reduce-scatter.3 | all-reduce-scatter fusion | flops 2310145 | bytes 11526656
  723.2 25.3 %all-gather.23.cloned.1.call-done = bf16[4,375,1536]{2,1,0:T(8,128)(2,1)} async-done(((bf16[1,375,1536]{2,1,0:T(8,128)(2,1)}), bf16[4,375,1536]{2,1,0:T(8,128)(2,1)}) %all-gather.23.cloned.1.call-update) | async-done | bytes 4608016 | tf_op jit(solution)/shard_map/all_gather | solution.py:261
  781.4 42.5 %fusion.4 = bf16[376,1536]{1,0:T(8,128)(2,1)S(1)} fusion(bf16[1500,1536]{1,0:T(8,128)(2,1)} %fusion.52), kind=kCustom, calls=%all-reduce-scatter.4 | all-reduce-scatter fusion | flops 2310145 | bytes 5763584
  940.7 194.2 %while.28 = (s32[]{:T(128)}, f32[1500,6,64]{0,2,1:T(8,128)}, f32[1500,6,64]{0,2,1:T(8,128)}, bf16[2,750,6,64]{1,3,2,0:T(8,128)(2,1)}, bf16[2,750,6,64]{1,3,2,0:T...) while((s32[]{:T(128)}, f32[1500,6,64]{0,2,1:T(8,128)}, ...), condition=%wide.region_24.25_spmd.clone, body=%wide.region_22.24_spmd.clone.sunk | while | flops 4385039360 | bytes 227283488 | solution.py:316
  943.9 14.5 fusion.407
  958.4 24.4 %multiply_reduce_fusion.7 = (f32[6,750]{1,0:T(8,128)}, f32[6,750,1500]{2,1,0:T(8,128)}) fusion(f32[6,750,1500]{2,1,0:T(8,128)} %fusion.407, f32[6,750]{1,0:T(8,128)S(1)} %dynamic-slice_bitcast_fusion.50, bf16[1500,6,64]{0,2,1:T(8,128)(2,1)S(1)} %get-tuple-element.462, bf16[2,750,6,64]{1,3,2,0:T(8,128)(2,1)S(1)} %copy-done.6, s32[]{:T(128)S(6)} %copy.119, ...), kind=kOutput, calls=%fused_computation.19.clone.1 | convolution fusion | flops 897745536 | bytes 56967124 | tf_op jit(solution)/shard_map/while/body/eval_jaxpr/qhe,khe->hqk/dot_general | solution.py:38
  982.8 22.5 %multiply_convert_fusion.4 = bf16[6,750,1500]{2,1,0:T(8,128)(2,1)} fusion(f32[6,750,1500]{2,1,0:T(8,128)} %get-tuple-element.406, f32[6,750,1500]{2,1,0:T(8,128)} %fusion.407, f32[6,750]{1,0:T(8,128)} %get-tuple-element.407), kind=kLoop, calls=%fused_computation.18.clone.1 | loop fusion | flops 20250000 | bytes 67518000 | tf_op jit(solution)/shard_map/while/body/eval_jaxpr/convert_element_type | solution.py:47
  1005.3 13.0 fusion.409
  1040.0 14.5 fusion.407
  1054.5 24.4 %multiply_reduce_fusion.7 = (f32[6,750]{1,0:T(8,128)}, f32[6,750,1500]{2,1,0:T(8,128)}) fusion(f32[6,750,1500]{2,1,0:T(8,128)} %fusion.407, f32[6,750]{1,0:T(8,128)S(1)} %dynamic-slice_bitcast_fusion.50, bf16[1500,6,64]{0,2,1:T(8,128)(2,1)S(1)} %get-tuple-element.462, bf16[2,750,6,64]{1,3,2,0:T(8,128)(2,1)S(1)} %copy-done.6, s32[]{:T(128)S(6)} %copy.119, ...), kind=kOutput, calls=%fused_computation.19.clone.1 | convolution fusion | flops 897745536 | bytes 56967124 | tf_op jit(solution)/shard_map/while/body/eval_jaxpr/qhe,khe->hqk/dot_general | solution.py:38
  1078.9 22.5 %multiply_convert_fusion.4 = bf16[6,750,1500]{2,1,0:T(8,128)(2,1)} fusion(f32[6,750,1500]{2,1,0:T(8,128)} %get-tuple-element.406, f32[6,750,1500]{2,1,0:T(8,128)} %fusion.407, f32[6,750]{1,0:T(8,128)} %get-tuple-element.407), kind=kLoop, calls=%fused_computation.18.clone.1 | loop fusion | flops 20250000 | bytes 67518000 | tf_op jit(solution)/shard_map/while/body/eval_jaxpr/convert_element_type | solution.py:47
  1101.5 13.7 fusion.409
  1225.1 23.9 %mul.436 = f32[1179648]{0:T(1024)} reshape(f32[6,8,1536,16]{3,2,1,0:T(8,128)} %broadcast_multiply_fusion) | data formatting | bytes 9437184 | tf_op jit(solution)/shard_map/mul | solution.py:88
  1267.4 424.7 %all-reduce.20 = (bf16[1966080]{0:T(1024)(128)(2,1)}, bf16[786432]{0:T(1024)(128)(2,1)}) all-reduce(f32[1966080]{0:T(1024)} %pad_maximum_fusion, f32[786432]{0:T(1024)} %pad_maximum_fusion.1), channel_id=9, replica_groups=mesh['dp'=8,'tensor'=4] {'dp'}, use_global_device_ids=true, to_apply=%region_29.30.clone | all-reduce | flops 2752512 | bytes 16515072
  1713.3 84.8 %fusion.242 = (bf16[376,1536]{1,0:T(8,128)(2,1)}, bf16[376,1536]{1,0:T(8,128)(2,1)}) fusion(bf16[1500,1536]{1,0:T(8,128)(2,1)} %fusion.51, bf16[1500,1536]{1,0:T(8,128)(2,1)} %fusion.53), kind=kCustom, calls=%all-reduce-scatter.6 | all-reduce-scatter fusion | flops 4620289 | bytes 11526656
  1858.7 27.5 %all-gather.13.cloned.1.call-done = bf16[1966080]{0:T(1024)(128)(2,1)} async-done(((bf16[245760]{0:T(1024)(128)(2,1)}), bf16[1966080]{0:T(1024)(128)(2,1)}) %all-gather.13.cloned.1.call-update) | async-done | bytes 3932176 | tf_op jit(solution)/shard_map/all_gather | solution.py:366
  1908.0 21.8 %slice.270 = f32[6,8,1536,16]{3,2,1,0:T(8,128)} reshape(f32[1179648]{0:T(1024)} %slice.285) | data formatting | bytes 9437184 | tf_op jit(solution)/shard_map/slice | solution.py:99
  1929.8 21.9 %copy.90 = f32[6,8,1536,16]{2,3,1,0:T(8,128)} copy(f32[6,8,1536,16]{3,2,1,0:T(8,128)} %slice.270) | data formatting | bytes 9437184
  (517 shorter events, 662.4 us)
Async XLA Ops:
  7.2 67.8 %copy-start = (bf16[6,8,1536,16]{2,3,1,0:T(8,128)(2,1)S(1)}, bf16[6,8,1536,16]{2,3,1,0:T(8,128)(2,1)}, u32[]{:S(2)}) copy-start(bf16[6,8,1536,16]{2,3,1,0:T(8,128)(2,1)} %param.29) | copy-start | bytes 7077892
  7.2 46.3 %all-gather.17.cloned.1.call-start = ((), (), s32[]{:S(2)}) async-start(), calls=%async_computation.5 | async-start | bytes 5775360 | tf_op jit(solution)/shard_map/all_gather | solution.py:175
  15.0 334.0 %all-gather.19.cloned.1.call-start = ((), (), s32[]{:S(2)}) async-start(), calls=%async_computation.6 | async-start | bytes 5775360 | tf_op jit(solution)/shard_map/all_gather | solution.py:198
  132.0 13.3 copy-start.76
  172.9 13.3 copy-start.76
  207.2 87.6 %copy-start.113 = (u32[32]{0:T(128)S(1)}, u32[32]{0:T(128)}, u32[]{:S(2)}) copy-start(u32[32]{0:T(128)} %constant.174) | copy-start | bytes 388
  290.4 5.7 collective-permute-start
  310.3 214.4 %all-gather.21.cloned.1.call-start = ((), (), s32[]{:S(2)}) async-start(), calls=%async_computation.7 | async-start | bytes 5775360 | tf_op jit(solution)/shard_map/all_gather | solution.py:217
  466.2 5.3 collective-permute-start.1
  485.7 262.7 %all-gather.23.cloned.1.call-start = ((), (), s32[]{:S(2)}) async-start(), calls=%async_computation.8 | async-start | bytes 5775360 | tf_op jit(solution)/shard_map/all_gather | solution.py:261
  489.4 82.7 %copy-start.73 = (f32[16,1500]{1,0:T(8,128)}, f32[16,1500]{1,0:T(8,128)S(1)}, u32[]{:S(2)}) copy-start(f32[16,1500]{1,0:T(8,128)S(1)} %fusion.156) | copy-start | bytes 288004
  534.1 38.0 %slice-start.6 = ((s8[9240576]{0:T(1024)(128)(4,1)}), s8[4194304]{0:T(1024)(128)(4,1)S(1)}, s32[]{:S(2)}) async-start(s8[9240576]{0:T(1024)(128)(4,1)} %bitcast.493), calls=%async_computation.16 | async-start | bytes 8388608
  543.7 28.5 %slice-start.7 = ((s8[9240576]{0:T(1024)(128)(4,1)}), s8[4194304]{0:T(1024)(128)(4,1)S(1)}, s32[]{:S(2)}) async-start(s8[9240576]{0:T(1024)(128)(4,1)} %bitcast.493), calls=%async_computation.17 | async-start | bytes 8388608
  543.7 28.5 %slice-start.8 = ((s8[9240576]{0:T(1024)(128)(4,1)}), s8[851968]{0:T(1024)(128)(4,1)S(1)}, s32[]{:S(2)}) async-start(s8[9240576]{0:T(1024)(128)(4,1)} %bitcast.493), calls=%async_computation.18 | async-start | bytes 1703936
  685.7 5.3 collective-permute-start.3
  706.7 13.2 slice-start.4
  709.5 203.7 %all-gather.25.cloned.1.call-start = ((), (), s32[]{:S(2)}) async-start(), calls=%async_computation.9 | async-start | bytes 5775360 | tf_op jit(solution)/shard_map/all_gather | solution.py:304
  824.0 13.1 copy-start.38
  824.0 17.3 collective-permute-start.4
  856.9 947.0 %reduce-scatter.14.cloned.1.call-start = ((), (), s32[]{:S(2)}) async-start(), calls=%async_computation.1 | async-start | bytes 245760 | tf_op jit(solution)/shard_map/reduce_scatter | solution.py:296
  913.1 906.7 %all-reduce.19.cloned.1.call-start = ((), (), s32[]{:S(2)}) async-start(), calls=%async_computation.2 | async-start | bytes 983040 | tf_op jit(solution)/shard_map/psum | solution.py:361
  943.9 14.5 copy-start.6
  1040.0 14.5 copy-start.6
  1701.5 134.9 %all-gather.15.cloned.1.call-start = ((), (), s32[]{:S(2)}) async-start(), calls=%async_computation.4 | async-start | bytes 1769472 | tf_op jit(solution)/shard_map/all_gather | solution.py:363
  1713.2 172.9 %all-gather.13.cloned.1.call-start = ((), (), s32[]{:S(2)}) async-start(), calls=%async_computation.3 | async-start | bytes 4423680 | tf_op jit(solution)/shard_map/all_gather | solution.py:366
  1798.0 19.7 %copy-start.16 = (bf16[375,1536]{1,0:T(8,128)(2,1)S(1)}, bf16[375,1536]{1,0:T(8,128)(2,1)}, u32[]{:S(2)}) copy-start(bf16[375,1536]{1,0:T(8,128)(2,1)} %param.22) | copy-start | bytes 3456004
  1798.0 19.7 %copy-start.78 = (f32[1536]{0:T(1024)S(1)}, f32[1536]{0:T(1024)}, u32[]{:S(2)}) copy-start(f32[1536]{0:T(1024)} %copy-done.77) | copy-start | bytes 18436
  1798.0 19.7 %copy-start.86 = (f32[375]{0:T(512)S(1)}, f32[375]{0:T(512)}, u32[]{:S(2)}) copy-start(f32[375]{0:T(512)} %copy-done.85) | copy-start | bytes 4504
  1799.5 9.3 collective-permute-start.5
  1805.3 14.5 copy-start.108
  1806.7 13.2 copy-start.100
  1806.7 15.6 collective-permute-start.2
  (113 other events, 516.2 us)
Sparse Core Ops, SparseCore 0:
  15.1 38.4 all-gather.16
  310.4 38.5 all-gather.18
  485.9 38.7 all-gather.20
  709.6 38.7 all-gather.22
  857.0 36.7 all-gather.24
  913.2 19.1 reduce-scatter.13
  1701.6 32.1 all-reduce.18
  1736.8 44.0 all-gather.14
  1820.0 66.0 all-gather.12
where the time goes:
time: 1980 us; the launch traced here: 1960 us
  blocking collectives  797 us (40%)
  matrix products  530 us (27%)
  local copies, waits for them, and re-layouts  286 us (14%)
  other arithmetic  156 us (8%)
  waiting for transfers between devices  145 us (7%)
  starting transfers between devices  25.1 us (1%)
    unnamed x6, blocking collectives  797 us
    dot_general x40, matrix products, dot_high(): jnp.dot(former, latter, precision=HIGHEST_PRECISION, preferred_element_ty...  176 us
    unnamed x270, local copies, waits for them, and re-layouts  137 us
    dot_general x20, matrix products, times_trans(): lax.dot_general(former, latter, (((1,), (1,)), ((), ())), preferred_eleme...  79 us
    dot_general x4, matrix products, causal_scores(): jnp.einsum('qhe,khe->hqk', queries, all_keys, preferred_element_type=jnp....  75.1 us
    dot_general x20, matrix products, dot_low(): return jnp.dot(former, latter, preferred_element_type=jnp.float32)  68.3 us
    slice x14, local copies, waits for them, and re-layouts, unflatten_all(): results.append(vector[offset:offset + piece.size].reshape(piece.shape))  52.4 us
    mul x8, local copies, waits for them, and re-layouts, into_slots(): return jnp.expand_dims(gradient, slot_axis) * slot_mask.reshape(new_shape)  46.3 us
  transfers between devices with their start and end apart: 15, of which 7 were waited for; matrix products, arithmetic and copies ran while one was open for 31% of the time, Pallas kernels for 0%

commit v1 on v0

v1 whole, which is shorter than its diff:
```python
from functools import partial

import jax
import jax.numpy as jnp
from jax import lax
from jax.experimental import pallas as pl
from jax.experimental.pallas import tpu as pltpu
from jax.sharding import PartitionSpec as P

HEAD = 64
EPSILON = 1e-05
NEG = -1e30
BF = jnp.bfloat16
F32 = jnp.float32
C2 = 0.125 * 1.4426950408889634
SUB = 128
TILE = 256
VM = pltpu.VMEM
MESH = pl.DeviceIdType.MESH


def nn(a, b):
    return jnp.dot(a, b, preferred_element_type=F32)


def nt(a, b):
    return lax.dot_general(a, b, (((1,), (1,)), ((), ())), preferred_element_type=F32)


def tn(a, b):
    return lax.dot_general(a, b, (((0,), (0,)), ((), ())), preferred_element_type=F32)


def ring():
    t = lax.axis_index("tensor")
    core = lax.rem(t, 2)
    chip = t // 2
    p = t + 1 - 2 * core
    o = lax.rem(t + 2, 4)
    q = lax.rem(p + 2, 4)
    return t, chip, p, o, q


def meet(*others):
    barrier = pltpu.get_barrier_semaphore()
    for other in others:
        pl.semaphore_signal(barrier, inc=1, device_id={"tensor": other}, device_id_type=MESH)
    pl.semaphore_wait(barrier, len(others))


def send(src, dst, ssem, rsem, to):
    return pltpu.make_async_remote_copy(
        src, dst, ssem, rsem, device_id={"tensor": to}, device_id_type=MESH
    )


def rows(block, sub, lp):
    return pl.ds(pl.multiple_of(block * lp + sub * SUB, SUB), SUB)


def half_masks(n):
    lane = lax.broadcasted_iota(jnp.int32, (n, 128), 1)
    return lane < HEAD


class Gather:
    def __init__(self, own, held, ssem, rsem, lp):
        self.own, self.held, self.ssem, self.rsem, self.lp = own, held, ssem, rsem, lp
        self.t, self.chip, self.p, self.o, self.q = ring()
        self.subs = lp // SUB

    def near(self):
        block = pl.ds(pl.multiple_of(self.t * self.lp, SUB), self.lp)
        return send(self.own, self.held.at[block], self.ssem.at[0], self.rsem.at[0], self.p)

    def far(self, s):
        return send(
            self.own.at[pl.ds(s * SUB, SUB)],
            self.held.at[rows(self.t, s, self.lp)],
            self.ssem.at[1 + s],
            self.rsem.at[1 + s],
            self.o,
        )

    def onward(self, s):
        piece = self.held.at[rows(self.o, s, self.lp)]
        k = 1 + self.subs + s
        return send(piece, piece, self.ssem.at[k], self.rsem.at[k], self.p)

    def start(self):
        for s in range(self.subs):
            self.far(s).start()
        self.near().start()

    def finish(self):
        self.near().wait_send()
        for s in range(self.subs):
            self.far(s).wait_send()
            self.onward(s).wait_send()


class Scatter:
    def __init__(self, result, out_p, in_p, out_x, in_x, sems, lp):
        self.result, self.out_p, self.in_p, self.out_x, self.in_x = result, out_p, in_p, out_x, in_x
        self.sp, self.rp, self.sx, self.rx = sems
        self.lp = lp
        self.t, self.chip, self.p, self.o, self.q = ring()
        self.subs = lp // SUB

    def pair(self, k):
        return send(self.out_p.at[k], self.in_p.at[k], self.sp.at[k], self.rp.at[k], self.p)

    def across(self, s):
        return send(self.out_x.at[s], self.in_x.at[s], self.sx.at[s], self.rx.at[s], self.o)

    def give(self, block, s, part):
        @pl.when(block == self.q)
        def _():
            self.out_p[s] = part[...].astype(self.out_p.dtype)
            self.pair(s).start()

        @pl.when(block == self.o)
        def _():
            self.pair(s).wait_recv()
            self.out_x[s] = (part[...] + self.in_p[s].astype(F32)).astype(BF)
            self.across(s).start()

        @pl.when(block == self.p)
        def _():
            self.out_p[self.subs + s] = part[...].astype(self.out_p.dtype)
            self.pair(self.subs + s).start()

        @pl.when(block == self.t)
        def _():
            self.result[pl.ds(pl.multiple_of(s * SUB, SUB), SUB), :] = part[...]

    def finish(self):
        for s in range(self.subs):
            self.pair(self.subs + s).wait_recv()
            self.across(s).wait_recv()
            r = pl.ds(s * SUB, SUB)
            self.result[r, :] += self.in_p[self.subs + s].astype(F32) + self.in_x[s].astype(F32)
        for s in range(self.subs):
            self.pair(s).wait_send()
            self.pair(self.subs + s).wait_send()
            self.across(s).wait_send()


def scatter_scratch(lp, width, near=BF):
    n = lp // SUB
    dma = pltpu.SemaphoreType.DMA
    return [
        VM((2 * n, SUB, width), near),
        VM((2 * n, SUB, width), near),
        VM((n, SUB, width), BF),
        VM((n, SUB, width), BF),
        dma((2 * n,)),
        dma((2 * n,)),
        dma((n,)),
        dma((n,)),
    ]


def make_scatter(result, scr, lp):
    return Scatter(result, scr[0], scr[1], scr[2], scr[3], scr[4:8], lp)


def tile_rows(i):
    return pl.ds(pl.multiple_of(i * TILE, TILE), TILE)


def fill_key_aux(kaux, lp, valid):
    n = kaux.shape[0]
    row = lax.broadcasted_iota(jnp.int32, (n, 128), 0)
    lane = lax.broadcasted_iota(jnp.int32, (n, 128), 1)
    pad = lax.rem(row, lp) >= valid
    kaux[...] = jnp.where(pad & (lane == 0), NEG, 0.0).astype(BF)


def first_lane():
    lane = lax.broadcasted_iota(jnp.int32, (TILE, 128), 1)
    return jnp.where(lane == 0, 1.0, 0.0).astype(BF)


def keep(mask, value):
    return jnp.where(mask, value, jnp.zeros_like(value))


def attend_tile(i, q_ref, k_ref, v_ref, att_ref, lse_ref, kaux, qa, ss, mx, acc):
    pairs = q_ref.shape[1] // 128
    left = half_masks(TILE)
    one = first_lane()
    ri = tile_rows(i)
    for p in range(pairs):
        qp = q_ref[ri, p * 128 : p * 128 + 128]
        for a in range(2):
            m = left if a == 0 else ~left
            qa[2 * p + a] = jnp.concatenate([keep(m, qp), one], axis=1)
            mx[2 * p + a] = jnp.full((TILE, 128), NEG, F32)

    def scores(j, diagonal):
        rj = tile_rows(j)
        for p in range(pairs):
            ka = jnp.concatenate([k_ref[rj, p * 128 : p * 128 + 128], kaux[rj, :]], axis=1)
            for a in range(2):
                s = nt(qa[2 * p + a], ka)
                if diagonal:
                    row = lax.broadcasted_iota(jnp.int32, (TILE, TILE), 0)
                    lane = lax.broadcasted_iota(jnp.int32, (TILE, TILE), 1)
                    s = jnp.where(lane > row, NEG, s)
                ss[2 * p + a, :, tile_rows(j)] = s
                mx[2 * p + a] = jnp.maximum(mx[2 * p + a], jnp.maximum(s[:, :128], s[:, 128:]))

    def body(j, carry):
        scores(j, False)
        return carry

    lax.fori_loop(0, i, body, 0)
    scores(i, True)
    for h in range(2 * pairs):
        mx[h] = jnp.broadcast_to(jnp.max(mx[h], axis=1, keepdims=True) * C2, (TILE, 128))
    for p in range(pairs):
        acc[p] = jnp.zeros((TILE, 256), F32)
    ones_l = jnp.where(left, 1.0, 0.0).astype(BF)
    ones_r = jnp.where(left, 0.0, 1.0).astype(BF)

    def mix(j, carry):
        rj = tile_rows(j)
        for p in range(pairs):
            pr = []
            for a in range(2):
                m = mx[2 * p + a]
                m2 = jnp.concatenate([m, m], axis=1)
                pr.append(jnp.exp2(ss[2 * p + a, :, tile_rows(j)] * C2 - m2).astype(BF))
            vp = v_ref[rj, p * 128 : p * 128 + 128]
            va = jnp.concatenate(
                [
                    jnp.concatenate([keep(left, vp), ones_l], axis=1),
                    jnp.concatenate([keep(~left, vp), ones_r], axis=1),
                ],
                axis=0,
            )
            acc[p] += nn(jnp.concatenate(pr, axis=1), va)
        return carry

    lax.fori_loop(0, i + 1, mix, 0)
    for p in range(pairs):
        total = acc[p, :, 128:]
        att_ref[ri, p * 128 : p * 128 + 128] = (acc[p, :, :128] / total).astype(BF)
        logs = jnp.where(left, mx[2 * p], mx[2 * p + 1]) + jnp.log2(total)
        flat = logs.T
        lse_ref[pl.ds(2 * p, 1), tile_rows(i)] = flat[0:1]
        lse_ref[pl.ds(2 * p + 1, 1), tile_rows(i)] = flat[64:65]


def stack_maps(maps):
    short = 64 - sum(m.shape[0] for m in maps)
    half = list(maps)
    if short:
        half = half + [jnp.zeros((short, maps[0].shape[1]), maps[0].dtype)]
    return jnp.concatenate(half + half, axis=0)


def block_maps(maps):
    n = len(maps)
    rows_ = []
    for j, m in enumerate(maps):
        parts = [jnp.zeros_like(m)] * n
        parts[j] = m
        rows_.append(jnp.concatenate(parts, axis=1))
    return stack_maps(rows_)


def split_rank(r):
    hi = r.astype(BF)
    lo = (r - hi.astype(F32)).astype(BF)
    return jnp.where(half_masks(r.shape[0]), hi, lo)


def layer_norm(x, gain, bias):
    mean = jnp.mean(x, axis=-1, keepdims=True)
    c = x - mean
    var = jnp.mean(c * c, axis=-1, keepdims=True)
    return c * lax.rsqrt(var + EPSILON) * gain + bias


def layer_norm_back(x, gain, dy):
    mean = jnp.mean(x, axis=-1, keepdims=True)
    c = x - mean
    var = jnp.mean(c * c, axis=-1, keepdims=True)
    inv = lax.rsqrt(var + EPSILON)
    xh = c * inv
    dg = dy * gain
    m1 = jnp.mean(dg, axis=-1, keepdims=True)
    m2 = jnp.mean(dg * xh, axis=-1, keepdims=True)
    return inv * (dg - m1 - xh * m2)


def self_forward_kernel(
    lp, pick_ref, x_ref, gain_ref, bias_ref, text_ref, colw, cola, cb_ref, roww, ra_ref, rb_ref,
    res_ref, q_ref, k_ref, v_ref, att_ref, lse_ref, rank_ref, xg, small, ca_ref,
    n1, wv, wkv, cav, w0, bx, b0, a0, qa, ss, mx, acc, kaux, pf, lsem, gs, gr, ms, mr, *scr
):
    g = Gather(n1, xg, gs, gr, lp)
    sc = make_scatter(res_ref, scr, lp)
    k = pick_ref[0]
    lw = q_ref.shape[1]
    d = n1.shape[1]
    tr = text_ref.shape[0]
    rk = cb_ref.shape[2]
    loads = [pltpu.make_async_copy(cola, cav, lsem.at[0])]
    for j in range(3):
        loads.append(pltpu.make_async_copy(colw.at[j], wv.at[:, pl.ds(j * lw, lw)], lsem.at[1 + j]))
    for j in range(2):
        loads.append(pltpu.make_async_copy(colw.at[4 + j], wkv.at[:, pl.ds(j * lw, lw)], lsem.at[4 + j]))
    loads.append(pltpu.make_async_copy(roww.at[0], w0, lsem.at[6]))
    for c in loads:
        c.start()
    meet(g.p, g.o, g.q)
    valid = x_ref.shape[0]
    for s in range(g.subs):
        lo, hi = s * SUB, min(valid, s * SUB + SUB)
        y = layer_norm(x_ref[lo:hi, :].astype(F32), gain_ref[0:1, :], bias_ref[0:1, :]).astype(BF)
        if hi < lo + SUB:
            n1[lo : lo + SUB, :] = jnp.zeros((SUB, d), BF)
        n1[lo:hi, :] = y
        g.far(s).start()
    g.near().start()
    fill_key_aux(kaux, lp, valid)
    lse_ref[...] = jnp.zeros_like(lse_ref)
    loads[0].wait()
    for j in range(cav.shape[0]):
        ca_ref[j] = cav[j, k]
    wv[:, 3 * lw :] = stack_maps([ca_ref[j] for j in range(3)]).T
    bx[...] = block_maps([cb_ref[j, k] for j in range(3)])
    b0[...] = stack_maps([rb_ref[0, k]])
    a0[...] = stack_maps([ra_ref[0, k]])
    for c in loads[1:]:
        c.wait()

    def project(r, x):
        y = nn(x, wv[...])
        e = split_rank(y[:, 3 * lw :])
        rank_ref[r, :] = e
        z = nn(e, bx[...])
        q_ref[r, :] = (y[:, :lw] + z[:, :lw]).astype(BF)
        k_ref[r, :] = (y[:, lw : 2 * lw] + z[:, lw : 2 * lw]).astype(BF)
        v_ref[r, :] = (y[:, 2 * lw : 3 * lw] + z[:, 2 * lw :]).astype(BF)

    tx = text_ref[...]
    e = split_rank(nt(tx, stack_maps([ca_ref[4], ca_ref[5]])))
    kv = nn(tx, wkv[...]) + nn(e, block_maps([cb_ref[4, k], cb_ref[5, k]]))
    small[g.t, :tr, :] = kv[:, :lw].astype(BF)
    small[g.t, tr : 2 * tr, :] = kv[:, lw:].astype(BF)
    small[g.t, 2 * tr : 2 * tr + rk, :] = cb_ref[3, k]
    small[g.t, 2 * tr + rk :, :] = ra_ref[1, k]

    def message(i, to):
        return send(small.at[g.t], small.at[g.t], ms.at[i], mr.at[i], to)

    message(0, g.p).start()
    message(1, g.o).start()
    message(2, g.q).start()

    r = pl.ds(pl.multiple_of(g.t * lp, SUB), lp)
    xg[r, :] = n1[...]
    project(r, n1[...])
    g.near().wait_recv()
    r = pl.ds(pl.multiple_of(g.p * lp, SUB), lp)
    project(r, xg[r, :])

    def arrive(s, carry):
        g.far(s).wait_recv()
        g.onward(s).start()
        r = rows(g.o, s, lp)
        project(r, xg[r, :])
        g.onward(s).wait_recv()
        r = rows(g.q, s, lp)
        project(r, xg[r, :])
        return carry

    lax.fori_loop(0, g.subs, arrive, 0)
    half = q_ref.shape[0] // (2 * TILE)

    def step(n, carry):
        second = n // half
        i = half * ((1 - g.chip) + second * (2 * g.chip - 1)) + lax.rem(n, half)
        attend_tile(i, q_ref, k_ref, v_ref, att_ref, lse_ref, kaux, qa, ss, mx, acc)
        a = att_ref[tile_rows(i), :]
        e = split_rank(nt(a, a0[...]))
        pf[...] = nn(a, w0[...]) + nn(e, b0[...])
        for c in range(TILE // SUB):
            chunk = i * (TILE // SUB) + c
            sc.give(chunk // g.subs, lax.rem(chunk, g.subs), pf.at[pl.ds(c * SUB, SUB)])
        return carry

    lax.fori_loop(0, 2 * half, step, 0)
    sc.finish()
    g.finish()
    for i, to in enumerate((g.p, g.o, g.q)):
        message(i, to).wait()


def vspec():
    return pl.BlockSpec(memory_space=VM)


def params(cid, vmem=60):
    return pltpu.CompilerParams(
        collective_id=cid, has_side_effects=True, vmem_limit_bytes=vmem * 2**20
    )


def cost(flops, nbytes):
    return pl.CostEstimate(flops=int(flops), bytes_accessed=int(nbytes), transcendentals=0)


def sspec():
    return pl.BlockSpec(memory_space=pltpu.SMEM)


def aspec():
    return pl.BlockSpec(memory_space=pl.ANY)


def self_forward(pick, x, gain, bias, text, colw, cola, cb, roww, ra, rb):
    valid, d = x.shape
    lp = -(-valid // SUB) * SUB
    lw = colw.shape[2]
    n = 4 * lp
    heads = lw // HEAD
    rk = cb.shape[2]
    sds = jax.ShapeDtypeStruct
    nsem = 1 + 2 * (lp // SUB)
    dma = pltpu.SemaphoreType.DMA
    return pl.pallas_call(
        partial(self_forward_kernel, lp),
        out_shape=[
            sds((lp, d), F32),
            sds((n, lw), BF),
            sds((n, lw), BF),
            sds((n, lw), BF),
            sds((n, lw), BF),
            sds((8, n), F32),
            sds((n, 128), BF),
            sds((n, d), BF),
            sds((4, 2 * text.shape[0] + 2 * rk, lw), BF),
            sds((cola.shape[0],) + cola.shape[2:], BF),
        ],
        in_specs=[sspec()] + [vspec()] * 4 + [aspec()] * 2 + [vspec()] + [aspec()] + [vspec()] * 2,
        out_specs=[vspec()] * 10,
        scratch_shapes=[
            VM((lp, d), BF),
            VM((d, 3 * lw + 128), BF),
            VM((d, 2 * lw), BF),
            VM(cola.shape, BF),
            VM((lw, d), BF),
            VM((128, 3 * lw), BF),
            VM((128, d), BF),
            VM((128, lw), BF),
            VM((heads, TILE, 256), BF),
            VM((heads, TILE, n), F32),
            VM((heads, TILE, 128), F32),
            VM((heads // 2, TILE, 256), F32),
            VM((n, 128), BF),
            VM((TILE, d), F32),
            dma((7,)),
            dma((nsem,)),
            dma((nsem,)),
            dma((3,)),
            dma((3,)),
        ]
        + scatter_scratch(lp, d, F32),
        compiler_params=params(1, 63),
        cost_estimate=cost(2 * n * d * 1280, n * d * 8),
        name="self_forward",
    )(pick, x, gain, bias, text, colw, cola, cb, roww, ra, rb)


def states(small, p, lo, n):
    per = small.shape[2] // 128
    x = small[p // per, lo : lo + n, pl.ds(pl.multiple_of(lax.rem(p, per) * 128, 128), 128)]
    left = half_masks(n)
    return jnp.concatenate([keep(left, x), keep(~left, x)], axis=0)


def whole_map(small, lo, n):
    return jnp.concatenate([small[i, lo : lo + n, :] for i in range(small.shape[0])], axis=1)


def pair_ones(n):
    left = half_masks(2 * n)
    row = lax.broadcasted_iota(jnp.int32, (2 * n, 128), 0)
    return jnp.where((row < n) == left, 1.0, 0.0).astype(BF)


def cross_scores(cqp, kst):
    s = nt(cqp, kst)
    left = half_masks(s.shape[0])
    m0 = jnp.max(jnp.where(left, s, NEG), axis=1, keepdims=True)
    m1 = jnp.max(jnp.where(left, NEG, s), axis=1, keepdims=True)
    return jnp.exp2((s - jnp.where(left, m0, m1)) * C2)


def cross_forward_kernel(
    tr, rk, pick_ref, out0_ref, x_ref, gain_ref, bias_ref, colw, roww, got, small, ca_ref, rb_ref,
    first_ref, n2_ref, cq_ref, cm_ref, second_ref, n3_ref, wcf, wrf, wc, wr, lsem, ssem, rsem, osem,
):
    t, chip, p, o, q = ring()
    k = pick_ref[0]
    lp, d = first_ref.shape
    valid = x_ref.shape[0]
    lw = wc.shape[2]
    share = got.shape[0]
    piece = got.shape[1] // 2

    def block(i):
        return pl.ds(pl.multiple_of(i * lw, 128), lw)

    mine = [pltpu.make_async_copy(colw.at[3], wc.at[t], lsem.at[0])]
    for i in range(share):
        mine.append(
            pltpu.make_async_copy(got.at[i, pl.ds(0, piece)], wc.at[o, pl.ds(i * piece, piece)], lsem.at[1 + i])
        )
    other = [pltpu.make_async_copy(roww.at[1], wr.at[block(t)], lsem.at[1 + share])]
    for i in range(share):
        col, row = i * piece // lw, i * piece % lw
        dst = wr.at[pl.ds(pl.multiple_of(o * lw + row, 64), piece), pl.ds(col * lw, lw)]
        other.append(pltpu.make_async_copy(got.at[i, pl.ds(piece, piece)], dst, lsem.at[2 + share + i]))
    for c in mine + other:
        c.start()
    meet(p)

    def swap(i):
        ref = (wc.at[t], wc.at[o], wr.at[block(t)], wr.at[block(o)])[i]
        return send(ref, ref, ssem.at[i], rsem.at[i], p)

    for s in range(lp // SUB):
        lo, hi = s * SUB, min(valid, s * SUB + SUB)
        if hi < lo + SUB:
            first_ref[lo : lo + SUB, :] = out0_ref[lo : lo + SUB, :]
        first_ref[lo:hi, :] = x_ref[lo:hi, :].astype(F32) + out0_ref[lo:hi, :]
        n2_ref[lo : lo + SUB, :] = layer_norm(
            first_ref[lo : lo + SUB, :], gain_ref[1:2, :], bias_ref[1:2, :]
        ).astype(BF)
        if s == 0:
            for c in mine:
                c.wait()
            swap(0).start()
            swap(1).start()
        if s == 1:
            for c in other:
                c.wait()
            swap(2).start()
            swap(3).start()
    n2 = n2_ref[...]
    e3 = split_rank(nt(n2, stack_maps([ca_ref[3]])))

    def project(i):
        b3 = stack_maps([small[i, 2 * tr : 2 * tr + rk, :]])
        cq_ref[:, block(i)] = (nn(n2, wc[i]) + nn(e3, b3)).astype(BF)

    project(t)
    project(o)
    swap(0).wait_recv()
    project(p)
    swap(1).wait_recv()
    project(q)
    ones = pair_ones(tr)

    def attend(j, carry):
        cols = pl.ds(pl.multiple_of(j * 128, 128), 128)
        pr = cross_scores(cq_ref[:, cols], states(small, j, 0, tr)).astype(BF)
        ov = nn(pr, jnp.concatenate([states(small, j, tr, tr), ones], axis=1))
        cm_ref[:, cols] = (ov[:, :128] / ov[:, 128:]).astype(BF)
        return carry

    lax.fori_loop(0, d // 128, attend, 0)
    swap(2).wait_recv()
    swap(3).wait_recv()
    keepc = [pltpu.make_async_copy(wc, wcf, osem.at[0]), pltpu.make_async_copy(wr, wrf, osem.at[1])]
    for c in keepc:
        c.start()
    cm = cm_ref[...]
    e1 = split_rank(nt(cm, stack_maps([whole_map(small, 2 * tr + rk, rk)])))
    second_ref[...] = first_ref[...] + nn(cm, wr[...]) + nn(e1, stack_maps([rb_ref[1, k]]))
    for s in range(lp // SUB):
        r = pl.ds(s * SUB, SUB)
        n3_ref[r, :] = layer_norm(second_ref[r, :], gain_ref[2:3, :], bias_ref[2:3, :]).astype(BF)
    for i in range(4):
        swap(i).wait_send()
    for c in keepc:
        c.wait()


def cross_forward(tr, rk, pick, out0, x, gain, bias, colw, roww, got, small, ca, rb):
    lp, d = out0.shape
    lw = colw.shape[2]
    share = got.shape[0]
    sds = jax.ShapeDtypeStruct
    dma = pltpu.SemaphoreType.DMA
    return pl.pallas_call(
        partial(cross_forward_kernel, tr, rk),
        out_shape=[
            sds((lp, d), F32),
            sds((lp, d), BF),
            sds((lp, d), BF),
            sds((lp, d), BF),
            sds((lp, d), F32),
            sds((lp, d), BF),
            sds((4, d, lw), BF),
            sds((4 * lw, d), BF),
        ],
        in_specs=[sspec()] + [vspec()] * 4 + [aspec()] * 3 + [vspec()] * 3,
        out_specs=[vspec()] * 6 + [aspec()] * 2,
        scratch_shapes=[
            VM((4, d, lw), BF),
            VM((4 * lw, d), BF),
            dma((2 + 2 * share,)),
            dma((4,)),
            dma((4,)),
            dma((2,)),
        ],
        compiler_params=params(4),
        cost_estimate=cost(4 * lp * d * d, 6 * d * d),
        name="cross_forward",
    )(pick, out0, x, gain, bias, colw, roww, got, small, ca, rb)


def cross_backward_kernel(
    tr, rk, pick_ref, gn3_ref, out3_ref, og_ref, second_ref, first_ref, n2_ref, cq_ref, cm_ref, gain_ref, wc_hbm, wr_hbm,
    small, ca_ref, rb_ref,
    gf_ref, gb_ref, dk_ref, dv_ref, a3g_ref, b3g_ref, a1g_ref, b1g_ref, block_ref,
    wc, wr, gs, g, gcm, dcq, gn2, lsem,
):
    loads = [
        pltpu.make_async_copy(wr_hbm, wr, lsem.at[0]),
        pltpu.make_async_copy(wc_hbm, wc, lsem.at[1]),
    ]
    for c in loads:
        c.start()
    k = pick_ref[0]
    lp, d = og_ref.shape
    for s in range(lp // SUB):
        r = pl.ds(s * SUB, SUB)
        v = og_ref[r, :].astype(F32) + layer_norm_back(second_ref[r, :], gain_ref[2:3, :], gn3_ref[r, :])
        gs[r, :] = v
        g[r, :] = v.astype(BF)
        ok = slice(s * SUB, min(block_ref.shape[0], s * SUB + SUB))
        block_ref[ok, :] = (second_ref[ok, :] + out3_ref[ok, :]).astype(BF)
    loads[0].wait()
    a1 = stack_maps([whole_map(small, 2 * tr + rk, rk)])
    b1 = stack_maps([rb_ref[1, k]])
    e1 = split_rank(nt(g[...], b1))
    gcm[...] = (nt(g[...], wr[...]) + nn(e1, a1)).astype(BF)
    ones = pair_ones(tr)

    def attend(j, carry):
        cols = pl.ds(pl.multiple_of(j * 128, 128), 128)
        kst = states(small, j, 0, tr)
        cqp, gp = cq_ref[:, cols], gcm[:, cols]
        pr = cross_scores(cqp, kst)
        pr = pr / nn(pr.astype(BF), ones)
        low = pr.astype(BF)
        dp = nt(gp, states(small, j, tr, tr))
        pd = pr * dp
        hi = pd.astype(BF)
        lo = (pd - hi.astype(F32)).astype(BF)
        mean = nn(jnp.concatenate([hi, lo], axis=1), jnp.concatenate([ones, ones], axis=0))
        ds = (pr * (dp - mean)).astype(BF)
        dcq[:, cols] = (nn(ds, kst) * 0.125).astype(BF)
        dk = tn(ds, cqp)
        dv = tn(low, gp)
        left = half_masks(tr)
        dk_ref[:, cols] = jnp.where(left, dk[:tr], dk[tr:]) * 0.125
        dv_ref[:, cols] = jnp.where(left, dv[:tr], dv[tr:])
        return carry

    lax.fori_loop(0, d // 128, attend, 0)
    loads[1].wait()
    lw = wc.shape[2]
    a3 = stack_maps([ca_ref[3]])
    e3 = split_rank(nt(dcq[...], stack_maps([whole_map(small, 2 * tr, rk)])))
    gn2[...] = nn(e3, a3)
    for t in range(wc.shape[0]):
        gn2[...] += nt(dcq[:, t * lw : t * lw + lw], wc[t])
    for s in range(lp // SUB):
        r = pl.ds(s * SUB, SUB)
        v = gs[r, :] + layer_norm_back(first_ref[r, :], gain_ref[1:2, :], gn2[r, :])
        gf_ref[r, :] = v
        gb_ref[r, :] = v.astype(BF)
    a3g_ref[...] = tn(e3, n2_ref[...])[:rk]
    b3g_ref[...] = tn(nt(n2_ref[...], a3).astype(BF), dcq[...])[:rk]
    a1g_ref[...] = tn(e1, cm_ref[...])[:rk]
    b1g_ref[...] = tn(nt(cm_ref[...], a1).astype(BF), g[...])[:rk]


def cross_backward(valid, tr, rk, pick, gn3, out3, og, second, first, n2, cq, cm, gain, wc, wr, small, ca, rb):
    lp, d = og.shape
    sds = jax.ShapeDtypeStruct
    return pl.pallas_call(
        partial(cross_backward_kernel, tr, rk),
        out_shape=[
            sds((lp, d), F32),
            sds((lp, d), BF),
            sds((tr, d), F32),
            sds((tr, d), F32),
        ]
        + [sds((rk, d), F32)] * 4 + [sds((valid, d), BF)],
        in_specs=[sspec()] + [vspec()] * 9 + [aspec()] * 2 + [vspec()] * 3,
        out_specs=[vspec()] * 9,
        scratch_shapes=[
            VM(wc.shape, BF),
            VM(wr.shape, BF),
            VM((lp, d), F32),
            VM((lp, d), BF),
            VM((lp, d), BF),
            VM((lp, d), BF),
            VM((lp, d), F32),
            pltpu.SemaphoreType.DMA((3,)),
        ],
        compiler_params=pltpu.CompilerParams(vmem_limit_bytes=60 * 2**20),
        cost_estimate=cost(4 * lp * d * d, 6 * d * d),
        name="cross_backward",
    )(pick, gn3, out3, og, second, first, n2, cq, cm, gain, wc, wr, small, ca, rb)


def mlp_kernel(
    lp, pick_ref, n3_ref, og_hbm, win_hbm, wout_hbm, ia_hbm, ib_hbm, oa_hbm, ob_hbm,
    gn_ref, out_ref, iag_ref, ibg_ref, oag_ref, obg_ref, own_ref,
    xg, og, win, wout, wt, hid, gp, bro, pf, maps, lsem, gs, gr, *scr
):
    g = Gather(n3_ref, xg, gs, gr, lp)
    half = len(scr) // 2
    sc1 = make_scatter(gn_ref, scr[:half], lp)
    sc2 = make_scatter(out_ref, scr[half:], lp)
    loads = [
        pltpu.make_async_copy(wout_hbm, wout, lsem.at[0]),
        pltpu.make_async_copy(og_hbm, og, lsem.at[1]),
        pltpu.make_async_copy(win_hbm, win, lsem.at[2]),
    ]
    for i, m in enumerate((ia_hbm, ib_hbm, oa_hbm, ob_hbm)):
        loads.append(pltpu.make_async_copy(m, maps.at[i], lsem.at[3 + i]))
    k = pick_ref[0]
    for c in loads:
        c.start()
    meet(g.p, g.o)
    g.start()
    n, d = xg.shape
    nb = n // lp
    for c in loads:
        c.wait()
    rk = maps.shape[2]
    ia, ib, oa, ob = maps[0, k], maps[1, k], maps[2, k], maps[3, k]
    valid = og.shape[0] // nb
    cut = valid // SUB * SUB
    for b in range(nb):

        @pl.when(g.t == b)
        def _():
            own_ref[cut:, :] = jnp.zeros((lp - cut, d), BF)
            own_ref[:valid, :] = og[b * valid : b * valid + valid, :]

    for c in range(wout.shape[0] // 128):
        r = slice(c * 128, c * 128 + 128)
        wout[r, :] = (wout[r, :].astype(F32) + tn(oa[:, r], ob)).astype(BF)
    obw = stack_maps([ob])
    ibw = stack_maps([ib])

    for b in range(nb):
        r = slice(b * lp, b * lp + valid)
        x = og[b * valid : b * valid + valid, :]
        gp[b * lp + cut : b * lp + lp, :] = jnp.zeros((lp - cut, gp.shape[1]), BF)
        gp[r, :] = nt(x, wout[...]).astype(BF)
        bro[b * lp + cut : b * lp + lp, :] = jnp.zeros((lp - cut, 128), BF)
        bro[r, :] = nt(x, obw).astype(BF)
    for c in range(win.shape[1] // 128):
        cs = slice(c * 128, c * 128 + 128)
        w = (win[:, cs].astype(F32) + tn(ia, ib[:, cs])).astype(BF)
        win[:, cs] = w
        wt[cs, :] = w.T
    wid = 256

    def inner(r, m):
        def col(c, carry):
            cs = pl.ds(pl.multiple_of(c * wid, wid), wid)
            pre = nn(xg[r, :], win[:, cs])
            cdf = 0.5 * lax.erf(pre * 0.7071067811865476) + 0.5
            slope = cdf + pre * (0.3989422804014327 * jnp.exp(-0.5 * pre * pre))
            hid[r, cs] = (pre * cdf).astype(BF)
            gp[r, cs] = (gp[r, cs].astype(F32) * slope).astype(BF)
            return carry

        lax.fori_loop(0, win.shape[1] // wid, col, 0)

    r = pl.ds(pl.multiple_of(g.t * lp, SUB), lp)
    xg[r, :] = n3_ref[...]
    inner(r, lp)
    g.near().wait_recv()
    r = pl.ds(pl.multiple_of(g.p * lp, SUB), lp)
    inner(r, lp)

    def arrive(s, carry):
        g.far(s).wait_recv()
        g.onward(s).start()
        inner(rows(g.o, s, lp), SUB)
        g.onward(s).wait_recv()
        inner(rows(g.q, s, lp), SUB)
        for b in (g.q, g.o):
            pf[...] = nn(gp[rows(b, s, lp), :], wt[...])
            sc1.give(b, s, pf)
        return carry

    lax.fori_loop(0, g.subs, arrive, 0)

    def near1(s, carry):
        for b in (g.p, g.t):
            pf[...] = nn(gp[rows(b, s, lp), :], wt[...])
            sc1.give(b, s, pf)
        return carry

    lax.fori_loop(0, g.subs, near1, 0)

    def far2(s, carry):
        for b in (g.q, g.o):
            pf[...] = nn(hid[rows(b, s, lp), :], wout[...])
            sc2.give(b, s, pf)
        return carry

    lax.fori_loop(0, g.subs, far2, 0)

    def near2(s, carry):
        for b in (g.p, g.t):
            pf[...] = nn(hid[rows(b, s, lp), :], wout[...])
            sc2.give(b, s, pf)
        return carry

    lax.fori_loop(0, g.subs, near2, 0)
    rank = nt(xg[...], stack_maps([ia])).astype(BF)
    ibg_ref[...] = tn(rank, gp[...])[:rk]
    iag_ref[...] = tn(nt(gp[...], ibw).astype(BF), xg[...])[:rk]
    oag_ref[...] = tn(bro[...], hid[...])[:rk]
    obg_ref[...] = jnp.zeros_like(obg_ref)
    oaw = stack_maps([oa])
    for b in range(nb):
        rank = nt(hid[b * lp : b * lp + valid, :], oaw).astype(BF)
        obg_ref[...] += tn(rank, og[b * valid : b * valid + valid, :])[:rk]
    sc1.finish()
    sc2.finish()
    g.finish()


def mlp(pick, n3, og, win, wout, ia, ib, oa, ob):
    lp, d = n3.shape
    f = win.shape[1]
    rk = ia.shape[1]
    n = 4 * lp
    sds = jax.ShapeDtypeStruct
    nsem = 1 + 2 * (lp // SUB)
    dma = pltpu.SemaphoreType.DMA
    return pl.pallas_call(
        partial(mlp_kernel, lp),
        out_shape=[
            sds((lp, d), F32),
            sds((lp, d), F32),
            sds((rk, d), F32),
            sds((rk, f), F32),
            sds((rk, f), F32),
            sds((rk, d), F32),
            sds((lp, d), BF),
        ],
        in_specs=[sspec(), vspec()] + [aspec()] * 7,
        out_specs=[vspec()] * 7,
        scratch_shapes=[
            VM((n, d), BF),
            VM(og.shape, BF),
            VM((d, f), BF),
            VM((f, d), BF),
            VM((f, d), BF),
            VM((n, f), BF),
            VM((n, f), BF),
            VM((n, 128), BF),
            VM((SUB, d), F32),
            VM((4,) + ia.shape, BF),
            dma((7,)),
            dma((nsem,)),
            dma((nsem,)),
        ]
        + scatter_scratch(lp, d)
        + scatter_scratch(lp, d),
        compiler_params=params(3, 63),
        cost_estimate=cost(8 * n * d * f, n * d * 16),
        name="mlp_both",
    )(pick, n3, og, win, wout, ia, ib, oa, ob)


def self_backward_kernel(
    lp, ndp, pick_ref, g_ref, roww, colw, ca_ref, cb_ref, ra_ref, rb_ref, q_ref, k_ref, v_ref, att_ref, lse_ref,
    n1_hbm, rank_ref, gain_ref, text_ref, x_ref, gf_hbm, dk_ref, dv_ref,
    a3g_ref, b3g_ref, a1g_ref, b1g_ref, iag_ref, ibg_ref, oag_ref, obg_ref,
    frames_ref, tg_ref, got_a, got_b, got_c, got_e, got_l,
    res_ref, gg, do, dqa, dka, dva, dqkv, kaux, delta,
    w0, wt, n1v, br0, br, ax, bx, a0, b0, pf,
    wkv, gkv, tsend, trecv, e1s, e1r, e2s, e2r, ls, lr, pa, pb, pc, eh, lh,
    lsem, gs, gr, ms, mr, ds_, dr, osem, xs, xr, *scr
):
    g = Gather(g_ref, gg, gs, gr, lp)
    sc = make_scatter(res_ref, scr, lp)
    k = pick_ref[0]
    lw = q_ref.shape[1]
    loads = [pltpu.make_async_copy(roww.at[0], w0, lsem.at[0])]
    for j in range(3):
        loads.append(pltpu.make_async_copy(colw.at[j], n1v.at[:, pl.ds(j * lw, lw)], lsem.at[1 + j]))
    later = pltpu.make_async_copy(n1_hbm, n1v, lsem.at[5])
    for j in range(2):
        loads.append(pltpu.make_async_copy(colw.at[4 + j], wkv.at[:, pl.ds(j * lw, lw)], lsem.at[6 + j]))
    valid = x_ref.shape[0]
    d = g_ref.shape[1]
    tr = text_ref.shape[0]
    rk = cb_ref.shape[2]
    tq = tr // 4
    me = lax.axis_index("dp")
    core = lax.rem(g.t, 2)
    peers = ((g.p, 1 - core), (g.o, core), (g.q, 1 - core))
    he, hl = eh.shape[0], lh.shape[0]

    def to_peers(kind, i):
        to, c = peers[i]
        if kind == 0:
            src, dst = e1s.at[to], e1r.at[g.t]
        elif kind == 1:
            src, dst = e2s.at[pl.ds(pl.multiple_of(c * he, 16), he)], e2r.at[g.t]
        elif kind == 2:
            src, dst = tsend.at[pl.ds(pl.multiple_of(to * tq, 16), tq)], trecv.at[g.t]
        else:
            src, dst = ls.at[pl.ds(pl.multiple_of(c * hl, 16), hl)], lr.at[g.t]
        return send(src, dst, ms.at[kind, i], mr.at[kind, i], to)

    pushes = (
        (pa, got_a.at[me]),
        (pb, got_b.at[me]),
        (pc, got_c.at[me]),
        (eh, got_e.at[core, me]),
        (lh, got_l.at[core, me]),
    )

    def push(kind, i):
        src, dst = pushes[kind]
        to = lax.rem(me + i, ndp)
        return pltpu.make_async_remote_copy(
            src, dst, ds_.at[kind, i], dr.at[kind, i], device_id={"dp": to}, device_id_type=MESH
        )

    def push_all(kind):
        src, dst = pushes[kind]
        pltpu.make_async_copy(src, dst, osem.at[kind]).start()

        def one_push(i, carry):
            push(kind, i).start()
            return carry

        lax.fori_loop(1, ndp, one_push, 0)

    def pushed(kind):
        src, dst = pushes[kind]
        pltpu.make_async_copy(src, dst, osem.at[kind]).wait()

        def one_wait(i, carry):
            push(kind, i).wait()
            return carry

        lax.fori_loop(1, ndp, one_wait, 0)

    def to_partner(kind):
        ref = (got_e, got_l)[kind].at[core]
        return send(ref, ref, xs.at[kind], xr.at[kind], g.p)
    for c in loads:
        c.start()
    barrier = pltpu.get_barrier_semaphore()
    for other, _ in peers:
        pl.semaphore_signal(barrier, inc=1, device_id={"tensor": other}, device_id_type=MESH)

    def greet(i, carry):
        pl.semaphore_signal(barrier, inc=1, device_id={"dp": lax.rem(me + i, ndp)}, device_id_type=MESH)
        return carry

    lax.fori_loop(1, ndp, greet, 0)
    pl.semaphore_wait(barrier, 3 + ndp - 1)
    g.start()
    for i in range(4):
        c = slice(i * lw, i * lw + lw)
        e1s[i, :tr, :] = dk_ref[:, c].astype(BF)
        e1s[i, tr : 2 * tr, :] = dv_ref[:, c].astype(BF)
        e1s[i, 2 * tr : 2 * tr + rk, :] = b3g_ref[:, c].astype(BF)
        e1s[i, 2 * tr + rk :, :] = a1g_ref[:, c].astype(BF)
    for i in range(3):
        to_peers(0, i).start()
    pa[:rk, :] = ibg_ref[...].astype(BF)
    pa[rk:, :] = oag_ref[...].astype(BF)
    push_all(0)
    n = q_ref.shape[0]
    pairs = lw // 128
    fill_key_aux(kaux, lp, valid)
    left = half_masks(TILE)
    one = first_lane()
    dqa[...] = jnp.zeros_like(dqa)
    delta[...] = jnp.zeros_like(delta)

    a0[...] = stack_maps([ra_ref[0, k]])
    b0[...] = stack_maps([rb_ref[0, k]])
    bx[...] = block_maps([cb_ref[j, k] for j in range(3)])
    loads[0].wait()

    def back(r, x):
        e = split_rank(nt(x, b0[...]))
        br0[r, :] = e
        do[r, :] = (nt(x, w0[...]) + nn(e, a0[...])).astype(BF)

    r = pl.ds(pl.multiple_of(g.t * lp, SUB), lp)
    gg[r, :] = g_ref[...]
    back(r, g_ref[...])
    g.near().wait_recv()
    r = pl.ds(pl.multiple_of(g.p * lp, SUB), lp)
    back(r, gg[r, :])
    for c in loads[1:]:
        c.wait()
    ax[...] = stack_maps([ca_ref[j] for j in range(3)])
    for c in range(3 * lw // 128):
        wt[c * 128 : c * 128 + 128, :] = n1v[:, c * 128 : c * 128 + 128].T
    later.start()

    def arrive(s, carry):
        g.far(s).wait_recv()
        g.onward(s).start()
        g.onward(s).wait_recv()
        return carry

    lax.fori_loop(0, g.subs, arrive, 0)
    for b in (g.o, g.q):
        r = pl.ds(pl.multiple_of(b * lp, SUB), lp)
        back(r, gg[r, :])
    lane = lax.broadcasted_iota(jnp.int32, (8, 128), 1)
    row = lax.broadcasted_iota(jnp.int32, (8, 128), 0)
    pick = jnp.where((lane // HEAD) == row, 1.0, 0.0).astype(BF)
    pick = jnp.concatenate([pick, pick], axis=1)

    def deltas(i, carry):
        r = tile_rows(i)
        for p in range(pairs):
            cols = slice(p * 128, p * 128 + 128)
            pr = do[r, cols].astype(F32) * att_ref[r, cols].astype(F32)
            hi = pr.astype(BF)
            lo = (pr - hi.astype(F32)).astype(BF)
            both = nt(pick, jnp.concatenate([hi, lo], axis=1))
            delta[pl.ds(2 * p, 2), r] = both[0:2]
        return carry

    lax.fori_loop(0, n // TILE, deltas, 0)

    own = pl.ds(pl.multiple_of(g.t * lw, 128), lw)

    def first_stage():
        for i in range(3):
            to_peers(0, i).wait_recv()
        near = [e1r[to] for to, _ in peers]

        def total(ref, lo, hi):
            y = ref[:, own]
            for b in near:
                y = y + b[lo:hi, :].astype(F32)
            return y

        gkv[:, :lw] = total(dk_ref, 0, tr).astype(BF)
        gkv[:, lw:] = total(dv_ref, tr, 2 * tr).astype(BF)
        pb[:rk, :] = total(b3g_ref, 2 * tr, 2 * tr + rk).astype(BF)
        pb[3 * rk : 4 * rk, :] = total(a1g_ref, 2 * tr + rk, 2 * tr + 2 * rk).astype(BF)
        tx = text_ref[...]
        a45 = stack_maps([ca_ref[4], ca_ref[5]])
        e = split_rank(nt(gkv[...], block_maps([cb_ref[4, k], cb_ref[5, k]])))
        tsend[...] = (nt(gkv[...], wkv[...]) + nn(e, a45)).astype(BF)
        ag45 = tn(e, tx)
        bg45 = tn(nt(tx, a45).astype(BF), gkv[...])
        pb[rk : 2 * rk, :] = bg45[:rk, :lw].astype(BF)
        pb[2 * rk : 3 * rk, :] = bg45[rk : 2 * rk, lw:].astype(BF)
        r0 = nt(att_ref[...], a0[...]).astype(BF)
        pb[4 * rk : 5 * rk, :] = tn(br0[...], att_ref[...])[:rk].astype(BF)
        slot = lax.broadcasted_iota(jnp.int32, (pb.shape[0] - 5 * rk, lw), 0)
        pb[5 * rk :, :] = jnp.where(slot == k, 1.0, 0.0).astype(BF)
        terms = (a3g_ref[...], ag45[:rk], ag45[rk : 2 * rk], tn(r0, gg[...])[:rk], b1g_ref[...], iag_ref[...], obg_ref[...])
        for i, m in enumerate(terms):
            e2s[i * rk : i * rk + rk, :] = m.astype(BF)
        e2s[len(terms) * rk :, :] = jnp.zeros((e2s.shape[0] - len(terms) * rk, d), BF)
        for i in range(3):
            to_peers(1, i).start()
            to_peers(2, i).start()

    def second_stage():
        for i in range(3):
            to_peers(1, i).wait_recv()
            to_peers(2, i).wait_recv()
        y = e2s[pl.ds(pl.multiple_of(core * he, 16), he), :].astype(F32)
        z = tsend[pl.ds(pl.multiple_of(g.t * tq, 16), tq), :].astype(F32)
        for to, _ in peers:
            y = y + e2r[to].astype(F32)
            z = z + trecv[to].astype(F32)
        eh[...] = y.astype(BF)
        tg_ref[...] = z
        push_all(1)
        push_all(3)

    def column(j, carry):
        pl.when(j == 1)(first_stage)
        pl.when(j == 2)(second_stage)
        rj = tile_rows(j)
        dka[...] = jnp.zeros_like(dka)
        dva[...] = jnp.zeros_like(dva)

        def block(i, diagonal):
            ri = tile_rows(i)
            for p in range(pairs):
                cols = slice(p * 128, p * 128 + 128)
                kp, vp, qp, dop = k_ref[rj, cols], v_ref[rj, cols], q_ref[ri, cols], do[ri, cols]
                qx = jnp.concatenate([qp, one], axis=1)
                aux = kaux[rj, :]
                pts, dss = [], []
                for a in range(2):
                    m = left if a == 0 else ~left
                    h = 2 * p + a
                    st = nt(jnp.concatenate([keep(m, kp), aux], axis=1), qx)
                    if diagonal:
                        kr = lax.broadcasted_iota(jnp.int32, (TILE, TILE), 0)
                        qc = lax.broadcasted_iota(jnp.int32, (TILE, TILE), 1)
                        st = jnp.where(kr > qc, NEG, st)
                    dp = nt(keep(m, vp), dop)
                    pt = jnp.exp2(st * C2 - lse_ref[pl.ds(h, 1), ri])
                    pts.append(pt.astype(BF))
                    dss.append((pt * (dp - delta[pl.ds(h, 1), ri])).astype(BF))
                do2 = jnp.concatenate([keep(left, dop), keep(~left, dop)], axis=0)
                q2 = jnp.concatenate([keep(left, qp), keep(~left, qp)], axis=0)
                k2 = jnp.concatenate([keep(left, kp), keep(~left, kp)], axis=0)
                dva[:, cols] += nn(jnp.concatenate(pts, axis=1), do2)
                dka[:, cols] += nn(jnp.concatenate(dss, axis=1), q2)
                dqa[ri, cols] += tn(jnp.concatenate(dss, axis=0), k2)

        block(j, True)

        def body(i, c):
            block(i, False)
            return c

        lax.fori_loop(j + 1, n // TILE, body, 0)
        dqkv[rj, lw : 2 * lw] = (dka[...] * 0.125).astype(BF)
        dqkv[rj, 2 * lw :] = dva[...].astype(BF)
        return carry

    lax.fori_loop(0, n // TILE, column, 0)

    def close(i, carry):
        r = tile_rows(i)
        dqkv[r, :lw] = (dqa[r, :] * 0.125).astype(BF)
        return carry

    lax.fori_loop(0, n // TILE, close, 0)

    br[...] = split_rank(nt(dqkv[...], bx[...]))
    later.wait()
    ls[...] = tn(br[...], n1v[...])[: ls.shape[0]].astype(BF)
    cbg = tn(rank_ref[...], dqkv[...])
    for j in range(3):
        pc[j * rk : j * rk + rk, :] = cbg[j * rk : j * rk + rk, j * lw : j * lw + lw].astype(BF)
    for i in range(3):
        to_peers(3, i).start()
    push_all(2)

    def term(b, s):
        r = rows(b, s, lp)
        pf[...] = nn(dqkv[r, :], wt[...]) + nn(br[r, :], ax[...])
        sc.give(b, s, pf)

    def step(s, carry):
        for b in (g.q, g.o):
            term(b, s)
        return carry

    lax.fori_loop(0, g.subs, step, 0)

    for i in range(3):
        to_peers(3, i).wait_recv()
    y = ls[pl.ds(pl.multiple_of(core * hl, 16), hl), :].astype(F32)
    for to, _ in peers:
        y = y + lr[to].astype(F32)
    lh[...] = y.astype(BF)
    push_all(4)

    def step2(s, carry):
        for b in (g.p, g.t):
            term(b, s)
        return carry

    lax.fori_loop(0, g.subs, step2, 0)
    pushed(3)
    to_partner(0).start()
    sc.finish()
    for s in range(lp // SUB):
        bring = pltpu.make_async_copy(gf_hbm.at[pl.ds(s * SUB, SUB)], pf, lsem.at[4])
        bring.start()
        bring.wait()
        r = slice(s * SUB, min(valid, s * SUB + SUB))
        frames_ref[r, :] = pf[: r.stop - r.start, :] + layer_norm_back(x_ref[r, :].astype(F32), gain_ref[0:1, :], res_ref[r, :])
    pushed(4)
    to_partner(1).start()
    g.finish()
    for kind in range(4):
        for i in range(3):
            to_peers(kind, i).wait_send()
    for kind in range(3):
        pushed(kind)
    to_partner(0).wait()
    to_partner(1).wait()


def self_backward(
    ndp, pick, g, roww, colw, ca, cb, ra, rb, q, k, v, att, lse, n1g, rank, x, gain, gf, text, dk, dv, grads
):
    lp, d = g.shape
    n, lw = q.shape
    valid = x.shape[0]
    tr = text.shape[0]
    rk, slots = cb.shape[2], cb.shape[1]
    he, hl = 4 * rk, 2 * rk
    sds = jax.ShapeDtypeStruct
    nsem = 1 + 2 * (lp // SUB)
    dma = pltpu.SemaphoreType.DMA
    nb = 5 * rk + slots
    return pl.pallas_call(
        partial(self_backward_kernel, lp, ndp),
        out_shape=[
            sds((valid, d), F32),
            sds((tr // 4, d), F32),
            sds((ndp, 2 * rk, d), BF),
            sds((ndp, nb, lw), BF),
            sds((ndp, 3 * rk, lw), BF),
            sds((2, ndp, he, d), BF),
            sds((2, ndp, hl, d), BF),
        ],
        in_specs=[sspec(), vspec()] + [aspec()] * 2 + [vspec()] * 9 + [aspec()] + [vspec()] * 4 + [aspec()] + [vspec()] * 10,
        out_specs=[vspec()] * 2 + [aspec()] * 5,
        scratch_shapes=[
            VM((lp, d), F32),
            VM((n, d), BF),
            VM((n, lw), BF),
            VM((n, lw), F32),
            VM((TILE, lw), F32),
            VM((TILE, lw), F32),
            VM((n, 3 * lw), BF),
            VM((n, 128), BF),
            VM((8, n), F32),
            VM((lw, d), BF),
            VM((3 * lw, d), BF),
            VM((n, d), BF),
            VM((n, 128), BF),
            VM((n, 128), BF),
            VM((128, d), BF),
            VM((128, 3 * lw), BF),
            VM((128, lw), BF),
            VM((128, d), BF),
            VM((SUB, d), F32),
            VM((d, 2 * lw), BF),
            VM((tr, 2 * lw), BF),
            VM((tr, d), BF),
            VM((4, tr // 4, d), BF),
            VM((4, 2 * tr + 2 * rk, lw), BF),
            VM((4, 2 * tr + 2 * rk, lw), BF),
            VM((2 * he, d), BF),
            VM((4, he, d), BF),
            VM((2 * hl, d), BF),
            VM((4, hl, d), BF),
            VM((2 * rk, d), BF),
            VM((nb, lw), BF),
            VM((3 * rk, lw), BF),
            VM((he, d), BF),
            VM((hl, d), BF),
            dma((8,)),
            dma((nsem,)),
            dma((nsem,)),
            dma((4, 3)),
            dma((4, 3)),
            dma((5, ndp)),
            dma((5, ndp)),
            dma((5,)),
            dma((2,)),
            dma((2,)),
        ]
        + scatter_scratch(lp, d),
        compiler_params=params(2, 63),
        cost_estimate=cost(2 * n * d * 2560, n * d * 8),
        name="self_backward",
    )(pick, g, roww, colw, ca, cb, ra, rb, q, k, v, att, lse, n1g, rank, gain, text, x, gf, dk, dv, *grads)


def finish_kernel(
    rk, picks, ga, gb, gc, ge, gl,
    col_a, col_b, row_a, row_b, in_a, in_b, out_a, out_b,
):
    c = pl.program_id(0)
    k = picks[c]
    outs = (col_a, col_b, row_a, row_b, in_a, in_b, out_a, out_b)

    @pl.when(c == 0)
    def _():
        for o in outs:
            o[...] = jnp.zeros_like(o)

    def piece(ref, i):
        return ref[0, i * rk : i * rk + rk, :].astype(F32)

    def common(ref, i):
        per = ref.shape[2] // rk
        return ref[i // per, 0, (i % per) * rk : (i % per) * rk + rk, :].astype(F32)

    for j in range(3):
        col_a[j, k] += common(gl, j)
        col_b[j, k] += piece(gc, j)
        col_a[3 + j, k] += common(ge, j)
        col_b[3 + j, k] += piece(gb, j)
    row_b[0, k] += common(ge, 3)
    row_b[1, k] += common(ge, 4)
    in_a[k] += common(ge, 5)
    out_b[k] += common(ge, 6)
    row_a[1, k] += piece(gb, 3)
    row_a[0, k] += piece(gb, 4)
    in_b[k] += piece(ga, 0)
    out_a[k] += piece(ga, 1)


def finish(picks, ga, gb, gc, ge, gl, slots, rk, f):
    ndp, _, d = ga.shape
    lw = gb.shape[2]
    sds = jax.ShapeDtypeStruct
    shapes = [
        (6, slots, rk, d), (6, slots, rk, lw), (2, slots, rk, lw), (2, slots, rk, d),
        (slots, rk, d), (slots, rk, f), (slots, rk, f), (slots, rk, d),
    ]

    def one(x):
        return pl.BlockSpec((1,) + x.shape[1:], lambda c, p: (c, 0, 0))

    def two(x):
        return pl.BlockSpec((2, 1) + x.shape[2:], lambda c, p: (0, c, 0, 0))

    def whole(s):
        return pl.BlockSpec(s, lambda c, p: (0,) * len(s))

    return pl.pallas_call(
        partial(finish_kernel, rk),
        out_shape=[sds(s, F32) for s in shapes],
        grid_spec=pltpu.PrefetchScalarGridSpec(
            num_scalar_prefetch=1,
            grid=(ndp,),
            in_specs=[one(ga), one(gb), one(gc), two(ge), two(gl)],
            out_specs=[whole(s) for s in shapes],
        ),
        compiler_params=pltpu.CompilerParams(vmem_limit_bytes=60 * 2**20),
        cost_estimate=cost(1e6, 2e7),
        name="finish",
    )(picks, ga, gb, gc, ge, gl)


def local(
    frames_in,
    text_states,
    adapter_pick,
    out_grad,
    norm_gain,
    norm_bias,
    col_w,
    col_a,
    col_b,
    row_w,
    row_a,
    row_b,
    mlp_in,
    mlp_in_a,
    mlp_in_b,
    mlp_out,
    mlp_out_a,
    mlp_out_b,
):
    k = adapter_pick[0]
    nt_ = lax.axis_size("tensor")
    ndp = lax.axis_size("dp")
    slots = col_a.shape[1]
    valid, d = frames_in.shape
    lw = col_w.shape[2]
    rank = col_b.shape[2]
    tr = text_states.shape[0]
    cola = jnp.swapaxes(col_a, 2, 3)
    rowa = jnp.swapaxes(row_a, 2, 3)
    ia_all, oa_all = jnp.swapaxes(mlp_in_a, 1, 2), jnp.swapaxes(mlp_out_a, 1, 2)

    share = min(ndp, 8)
    piece = d // share
    part = lax.rem(lax.axis_index("dp"), share)
    stacked = jnp.swapaxes(row_w[1].reshape(lw, nt_, lw), 0, 1).reshape(d, lw)
    mine = jnp.concatenate(
        [lax.dynamic_slice_in_dim(col_w[3], part * piece, piece, 0), lax.dynamic_slice_in_dim(stacked, part * piece, piece, 0)],
        axis=0,
    )
    mine = lax.ppermute(mine, "tensor", [(i, (i + nt_ // 2) % nt_) for i in range(nt_)])
    groups = [[g * share + i for i in range(share)] for g in range(ndp // share)]
    got = lax.all_gather(mine, "dp", axis=0, tiled=False, axis_index_groups=groups)

    out0, q, kk, v, att, lse, ranks, n1g, small, ca = self_forward(
        adapter_pick, frames_in, norm_gain, norm_bias, text_states, col_w, cola, col_b, row_w, rowa, row_b
    )
    first, n2, cq, cm, second, n3, wc, wr = cross_forward(
        tr, rank, adapter_pick, out0, frames_in, norm_gain, norm_bias, col_w, row_w, got, small, ca, row_b
    )
    gn3, out3, iag, ibg, oag, obg, og_own = mlp(
        adapter_pick, n3, out_grad, mlp_in, mlp_out, ia_all, mlp_in_b, oa_all, mlp_out_b
    )
    gf, gb, dck, dcv, a3g, b3g, a1g, b1g, block_out = cross_backward(
        valid, tr, rank, adapter_pick, gn3, out3, og_own, second, first, n2, cq, cm, norm_gain, wc, wr, small, ca, row_b
    )
    frames_grad, text_grad, got_a, got_b, got_c, got_e, got_l = self_backward(
        ndp, adapter_pick, gb, row_w, col_w, ca, col_b, rowa, row_b, q, kk, v, att, lse, n1g, ranks,
        frames_in, norm_gain, gf, text_states, dck, dcv, (a3g, b3g, a1g, b1g, iag, ibg, oag, obg)
    )
    hot = got_b[:, 5 * rank :, 0].astype(F32)
    picks = jnp.sum(hot * lax.iota(F32, slots)[None, :], axis=1).astype(jnp.int32)
    col_a_grad, col_b_grad, row_a_grad, row_b_grad, in_a, in_b, out_a, out_b = finish(
        picks, got_a, got_b, got_c, got_e, got_l, slots, rank, mlp_in.shape[1]
    )
    col_a_grad = jnp.swapaxes(col_a_grad, 2, 3)
    row_a_grad = jnp.swapaxes(row_a_grad, 2, 3)
    mlp_in_a_grad, mlp_in_b_grad = jnp.swapaxes(in_a, 1, 2), in_b
    mlp_out_a_grad, mlp_out_b_grad = jnp.swapaxes(out_a, 1, 2), out_b
    return (
        block_out,
        frames_grad,
        text_grad,
        col_a_grad,
        col_b_grad,
        row_a_grad,
        row_b_grad,
        mlp_in_a_grad,
        mlp_in_b_grad,
        mlp_out_a_grad,
        mlp_out_b_grad,
    )


def solution(mesh):
    return jax.shard_map(
        local,
        mesh=mesh,
        in_specs=(
            P(("dp", "tensor"), None),
            P("dp", None),
            P("dp"),
            P("dp", None),
            P(),
            P(),
            P(None, None, "tensor"),
            P(),
            P(None, None, None, "tensor"),
            P(None, "tensor", None),
            P(None, None, "tensor", None),
            P(),
            P(None, "tensor"),
            P(),
            P(None, None, "tensor"),
            P("tensor", None),
            P(None, "tensor", None),
            P(),
        ),
        out_specs=(
            P(("dp", "tensor"), None),
            P(("dp", "tensor"), None),
            P(("dp", "tensor"), None),
            P(),
            P(None, None, None, "tensor"),
            P(None, None, "tensor", None),
            P(),
            P(),
            P(None, None, "tensor"),
            P(None, "tensor", None),
            P(),
        ),
        check_vma=False,
    )
```

time: 1980 us -> 402 us (0.20)
  blocking collectives: 797 us -> 0 us
  matrix products: 530 us -> 0 us
  Pallas kernels: 0 us -> 364 us
  local copies, waits for them, and re-layouts: 286 us -> 5.61 us
  other arithmetic: 156 us -> 1.48 us
  waiting for transfers between devices: 145 us -> 6.7 us
  starting transfers between devices: 25.1 us -> 1.31 us
    unnamed x6 -> x0, blocking collectives: 797 us -> none
    dot_general x99 -> x0, matrix products: 526 us -> none  [the longest x40 176 us: dot_high(): jnp.dot(former, latter, precision=HIGHEST_PRECISION, preferred_element_ty...]
    pallas_call x0 -> x6, Pallas kernels: none -> 364 us  [the longest x1 139 us: self_backward(): pl.pallas_call(partial(self_backward_kernel, lp, ndp), out_shape=[sds((va...]
    all_gather x7 -> x1, waiting for transfers between devices: 143 us -> 0.02 us  [local(): lax.all_gather(mine, 'dp', axis=0, tiled=False, axis_index_groups=groups)]
    unnamed x270 -> x8, local copies, waits for them, and re-layouts: 137 us -> 2.75 us
    slice x15 -> x4, local copies, waits for them, and re-layouts: 54 us -> 2.37 us  [the longest x2 1.27 us: local(): stacked = jnp.swapaxes(row_w[1].reshape(lw, nt_, lw), 0, 1).reshape(d, lw)]
    convert_element_type x8 -> x2, other arithmetic: 50.9 us -> 1.32 us  [the longest x1 0.8 us: local(): hot = got_b[:, 5 * rank:, 0].astype(F32)]
    reduce_sum x14 -> x1, other arithmetic: 47.8 us -> 0.12 us  [local(): jnp.sum(hot * lax.iota(F32, slots)[None, :], axis=1).astype(jnp.int32)]
  transfers between devices with their start and end apart: 15 -> 2, of which waited for: 7 -> 1; matrix products, arithmetic and copies ran while one was open for 31% -> 0% of each run, Pallas kernels for 0% -> 18%
where the time goes in v1:
time: 402 us; the launch traced here: 395 us
  Pallas kernels  364 us (91%)
  between operations  15.2 us (4%)
  waiting for transfers between devices  6.7 us (2%)
  local copies, waits for them, and re-layouts  5.61 us (1%)
    pallas_call x1, Pallas kernels, self_backward(): pl.pallas_call(partial(self_backward_kernel, lp, ndp), out_shape=[sds((va...  139 us
    pallas_call x1, Pallas kernels, mlp(): pl.pallas_call(partial(mlp_kernel, lp), out_shape=[sds((lp, d), F32), sds...  88.8 us
    pallas_call x1, Pallas kernels, self_forward(): pl.pallas_call(partial(self_forward_kernel, lp), out_shape=[sds((lp, d),...  72.7 us
    pallas_call x1, Pallas kernels, cross_backward(): pl.pallas_call(partial(cross_backward_kernel, tr, rk), out_shape=[sds((lp...  30.4 us
    pallas_call x1, Pallas kernels, cross_forward(): pl.pallas_call(partial(cross_forward_kernel, tr, rk), out_shape=[sds((lp,...  22.2 us
    pallas_call x1, Pallas kernels, finish(): pl.pallas_call(partial(finish_kernel, rk), out_shape=[sds(s, F32) for s i...  11.1 us
  transfers between devices with their start and end apart: 2, of which 1 were waited for; matrix products, arithmetic and copies ran while one was open for 0% of the time, Pallas kernels for 18%

profile of v1, /device:TPU:13, one launch (start us, length us, event | category | flops | bytes accessed | tf_op | source)
XLA Modules:
  0.0 394.6 jit_solution(14974378130007533007)
XLA Ops:
  7.2 0.0 all-gather.3.cloned.1.call-start
  7.2 0.0 slice-start.1
  7.2 1.3 slice-done.1
  8.5 0.3 reshape_squeeze.3
  8.8 0.0 slice-start
  8.8 0.2 copy.30
  9.0 1.1 slice-done
  10.2 1.3 collective-permute-start
  11.4 6.7 %collective-permute-done = bf16[384,384]{1,0:T(8,128)(2,1)S(1)} collective-permute-done((bf16[384,384]{1,0:T(8,128)(2,1)S(1)}, bf16[384,384]{1,0:T(8,128)(2,1)S(1)}, u32[]{:S(2)}, u32[]{:S(2)}) %collective-permute-start) | collective-permute-done | bytes 294944 | tf_op jit(solution)/shard_map/ppermute | solution.py:1409
  18.1 0.0 copy-start.1
  18.1 0.7 copy-done.1
  18.8 0.0 all-gather.3.cloned.1.call-update
  19.5 72.7 %self_forward.1 = (f32[384,1536]{1,0:T(8,128)}, bf16[1536,384]{1,0:T(8,128)(2,1)}, bf16[1536,384]{1,0:T(8,128)(2,1)}, bf16[1536,384]{1,0:T(8,128)(2,1)}, bf16[15...) custom-call(s32[1]{0:T(128)S(6)} %copy.33.pick_ref, ...), custom_call_target="tpu_custom_call" | custom-call | flops 6039797760 | bytes 18874368 | tf_op jit(solution)/shard_map/self_forward/pallas_call | solution.py:436
  92.2 0.0 all-gather.3.cloned.1.call-done
  92.3 22.2 %cross_forward.1 = (f32[384,1536]{1,0:T(8,128)}, bf16[384,1536]{1,0:T(8,128)(2,1)}, bf16[384,1536]{1,0:T(8,128)(2,1)}, bf16[384,1536]{1,0:T(8,128)(2,1)}, f32[38...) custom-call(s32[1]{0:T(128)S(6)} %copy.33.pick_ref, ...), custom_call_target="tpu_custom_call" | custom-call | flops 3623878656 | bytes 14155776 | tf_op jit(solution)/shard_map/cross_forward/pallas_call | solution.py:602
  114.5 88.8 %mlp_both.1 = (f32[384,1536]{1,0:T(8,128)}, f32[384,1536]{1,0:T(8,128)}, f32[16,1536]{1,0:T(8,128)}, f32[16,1536]{1,0:T(8,128)}, f32[16,1536]{1,0:T(8,128)}, /*i...) custom-call(s32[1]{0:T(128)S(6)} %copy.33.pick_ref, bf16[384,1536]{1,0:T(8,128)(2,1)} %get-tuple-element.63.n3_ref, ...), custom_call_target="tpu_custom_call" | custom-call | flops 28991029248 | bytes 37748736 | tf_op jit(solution)/shard_map/mlp_both/pallas_call | solution.py:861
  203.3 30.4 %cross_backward.1 = (f32[384,1536]{1,0:T(8,128)}, bf16[384,1536]{1,0:T(8,128)(2,1)}, f32[64,1536]{1,0:T(8,128)}, f32[64,1536]{1,0:T(8,128)}, f32[16,1536]{1,0:T(...) custom-call(s32[1]{0:T(128)S(6)} %copy.33.pick_ref, ...), custom_call_target="tpu_custom_call" | custom-call | flops 3623878656 | bytes 14155776 | tf_op jit(solution)/shard_map/cross_backward/pallas_call | solution.py:701
  233.7 139.0 %self_backward.1 = (f32[375,1536]{1,0:T(8,128)}, f32[16,1536]{1,0:T(8,128)}, bf16[8,32,1536]{2,1,0:T(8,128)(2,1)}, bf16[8,88,384]{2,1,0:T(8,128)(2,1)}, bf16[8,4...) custom-call(s32[1]{0:T(128)S(6)} %copy.33.pick_ref, ...), custom_call_target="tpu_custom_call" | custom-call | flops 12079595520 | bytes 18874368 | tf_op jit(solution)/shard_map/self_backward/pallas_call | solution.py:1235
  372.7 0.8 convert_reduce_fusion
  373.5 0.1 multiply_reduce_fusion
  373.6 0.5 convert_element_type.11.picks
  374.1 0.0 copy-start
  374.1 11.1 %finish.1 = (f32[6,8,16,1536]{3,2,1,0:T(8,128)}, f32[6,8,16,384]{3,2,1,0:T(8,128)}, f32[2,8,16,384]{3,2,1,0:T(8,128)}, f32[2,8,16,1536]{3,2,1,0:T(8,128)}, f32[8...) custom-call(s32[8]{0:T(128)} %convert_element_type.11.picks, ...), custom_call_target="tpu_custom_call" | custom-call | flops 1000000 | bytes 20000000 | tf_op jit(solution)/shard_map/finish/pallas_call | solution.py:1354
  385.3 0.0 copy-done
  385.3 0.0 copy-start.2
  385.3 1.4 copy.34
  386.7 0.0 copy-done.2
  386.7 0.6 copy.35
  (3 shorter events, 0.1 us)
Async XLA Ops:
  7.2 85.1 %all-gather.3.cloned.1.call-start = ((), (), s32[]{:S(2)}) async-start(), calls=%async_computation | async-start | bytes 2654208 | tf_op jit(solution)/shard_map/all_gather | solution.py:1411
  7.2 1.3 slice-start.1
  8.8 1.3 slice-start
  10.2 7.9 %collective-permute-start = (bf16[384,384]{1,0:T(8,128)(2,1)S(1)}, bf16[384,384]{1,0:T(8,128)(2,1)S(1)}, u32[]{:S(2)}, u32[]{:S(2)}) collective-permute-start(bf16[384,384]{1,0:T(8,128)(2,1)S(1)} %pad_maximum_fusion), channel_id=1, source_target_pairs={{0,2},{1,3},{2,0},{3,1},{4,6},{5,7},{6,4},{7,5},{8,10},{9,11},{10,... | collective-permute-start | bytes 884744 | tf_op jit(solution)/shard_map/ppermute | solution.py:1409
  18.1 0.7 copy-start.1
  374.1 11.1 %copy-start = (f32[375,1536]{1,0:T(8,128)S(1)}, f32[375,1536]{1,0:T(8,128)}, u32[]{:S(2)}) copy-start(f32[375,1536]{1,0:T(8,128)} %get-tuple-element.121) | copy-start | bytes 6912004
  385.3 1.4 copy-start.2
Sparse Core Ops, SparseCore 0:
  19.0 52.0 all-gather.2
